TPU v7x, 128 devices: a whole 4x4x4 slice. The times are simulated.
128 devices in a mesh: dp: 8 (over z, y_lo), pocket: 16 (over x, y_hi, core).
Axes of the slice: x: 4, y: 4 (y_hi: 2, y_lo: 2; y = y_hi * 2 + y_lo), z: 4, core: 2. Of those that a mesh axis runs over, the one named last changes fastest.
Arguments:
- atoms: bfloat16 [1024, 128, 768], P(('dp', 'pocket')), may hold values from -6 to 6
- distance_bins: int32 [1024, 128, 128], P(('dp', 'pocket')), may hold values from 0 to 31
- bonds: int32 [1024, 128, 128], P(('dp', 'pocket')), may hold values 0 or 1
- molecule: int32 [1024, 128], P(('dp', 'pocket')), may hold values from 0 to 3, never falling along the last dimension, each value on 1 to 64 neighbouring positions
- block_counts: int32 [8, 16], P('dp', 'pocket'), may hold values from 1 to 8, as said below
- block_scaffold: int32 [1024], replicated, may hold values from 0 to 8191
- pocket_ids: int32 [8192, 4], replicated, may hold values from 0 to 15, as said below
- pocket_keys: bfloat16 [2048, 768], P('pocket'), may hold values from -6 to 6
- pocket_values: bfloat16 [2048, 768], P('pocket'), may hold values from -6 to 6
- pocket_bias: bfloat16 [12, 2048], P(None, 'pocket'), may hold values from -4 to 320
- bin_table: float32 [12, 32], replicated, may hold values from -4 to 320
- bond_weight: float32 [12], replicated, may hold values from 0.5 to 2.5
- w_query: bfloat16 [768, 768], replicated, may hold values from -0.21875 to 0.21875
- w_key: bfloat16 [768, 768], replicated, may hold values from -0.21875 to 0.21875
- w_value: bfloat16 [768, 768], replicated, may hold values from -0.21875 to 0.21875
- w_out: bfloat16 [768, 768], replicated, may hold values from -0.21875 to 0.21875
- w_cross_query: bfloat16 [768, 768], replicated, may hold values from -0.21875 to 0.21875
- w_cross_out: bfloat16 [768, 768], replicated, may hold values from -0.21875 to 0.21875
- cotangent: bfloat16 [512, 128, 768], P(('dp', 'pocket')), may hold values from -6 to 6
Outputs:
- updated: bfloat16 [512, 128, 768], P(('dp', 'pocket'))
- weight_grads: bfloat16 [6, 768, 768], replicated
Inputs may be any that keep to these rules, and one draw needn't show every extreme that they name: `block_counts`: every column sums to 32, and in every column one device has exactly 8 live blocks. `pocket_ids`: each row names 4 different pocket blocks.
All inputs are finite; a program needn't handle non-finite values. No bound on the sum of `bonds` on one device may be relied on, other than what follows from the above.
Results may differ from a plain program's by a relative error of at most 0.012.
The roundings to bfloat16 on the way count: a program that leaves them out, or rounds other values in their place, can miss the bound.
Values may be sent and summed in bfloat16 or wider, within the bound.
No kernel may reach another device: no remote copies, remote signals or barrier semaphores. Data moves between devices by JAX's collectives and lax.ppermute only.
A program may use at most 128 MiB of HBM per device.

v0:
```python
import math

import jax
import jax.numpy as jnp
from jax import lax
from jax.sharding import PartitionSpec as P

masked_value = -30000.0


def pair_bias(bin_rows, bond_rows, molecule_rows, bin_table, bond_weight):
    bin_count = bin_table.shape[1]
    levels = lax.broadcasted_iota(jnp.int32, (1, 1, 1, bin_count), 3)
    one_hot = (bin_rows[..., None] == levels).astype(jnp.float32)
    looked_up = jnp.einsum("cijn,hn->chij", one_hot, bin_table, precision=lax.Precision.HIGHEST)
    bonded = looked_up + bond_weight[None, :, None, None] * bond_rows[:, None, :, :].astype(
        jnp.float32
    )
    same_molecule = molecule_rows[:, None, :, None] == molecule_rows[:, None, None, :]
    return jnp.where(same_molecule, bonded, masked_value).astype(jnp.bfloat16)


def project_rows(left, weight):
    flat = left.reshape(-1, left.shape[-1])
    result = jnp.dot(flat, weight, preferred_element_type=jnp.float32)
    return result.reshape(left.shape[:-1] + (weight.shape[1],))


def project_back(left, weight):
    flat = left.reshape(-1, left.shape[-1])
    result = lax.dot_general(
        flat, weight, (((1,), (1,)), ((), ())), preferred_element_type=jnp.float32
    )
    return result.reshape(left.shape[:-1] + (weight.shape[0],))


def weight_product(left, right):
    return lax.dot_general(
        left.reshape(-1, left.shape[-1]),
        right.reshape(-1, right.shape[-1]),
        (((0,), (0,)), ((), ())),
        preferred_element_type=jnp.float32,
    )


def softmax_rows(scores):
    highest = jnp.max(scores, axis=-1, keepdims=True)
    expsum = jnp.exp(scores - highest)
    return expsum / jnp.sum(expsum, axis=-1, keepdims=True)


def split_heads(matrix, heads):
    return matrix.reshape(matrix.shape[0], matrix.shape[1], heads, matrix.shape[2] // heads)


def einsum_mixed(form, left, right):
    return jnp.einsum(form, left, right, preferred_element_type=jnp.float32)


def layer_pass(
    block_atoms, block_bias, cross_keys, cross_values, cross_bias, cotangent_rows, weights, heads
):
    w_query, w_key, w_value, w_out, w_cquery, w_cout = weights
    block_count, row_count, width = block_atoms.shape
    scale = 1.0 / math.sqrt(width // heads)
    query_rows = project_rows(block_atoms, w_query).astype(jnp.bfloat16)
    key_rows = project_rows(block_atoms, w_key).astype(jnp.bfloat16)
    value_rows = project_rows(block_atoms, w_value).astype(jnp.bfloat16)
    query_heads = split_heads(query_rows, heads)
    key_heads = split_heads(key_rows, heads)
    value_heads = split_heads(value_rows, heads)
    scores = einsum_mixed("bihd,bjhd->bhij", query_heads, key_heads) * scale + block_bias.astype(
        jnp.float32
    )
    probs = softmax_rows(scores)
    probs_rounded = probs.astype(jnp.bfloat16)
    attended = (
        einsum_mixed("bhij,bjhd->bihd", probs_rounded, value_heads)
        .reshape(block_count, row_count, width)
        .astype(jnp.bfloat16)
    )
    middle = (block_atoms.astype(jnp.float32) + project_rows(attended, w_out)).astype(jnp.bfloat16)
    cross_query = project_rows(middle, w_cquery).astype(jnp.bfloat16)
    cquery_heads = split_heads(cross_query, heads)
    ckey_heads = split_heads(cross_keys, heads)
    cvalue_heads = split_heads(cross_values, heads)
    cross_scores = (
        einsum_mixed("bihd,bthd->bhit", cquery_heads, ckey_heads) * scale
        + cross_bias.astype(jnp.float32)[:, :, None, :]
    )
    cross_probs = softmax_rows(cross_scores)
    cross_rounded = cross_probs.astype(jnp.bfloat16)
    cross_attended = (
        einsum_mixed("bhit,bthd->bihd", cross_rounded, cvalue_heads)
        .reshape(block_count, row_count, width)
        .astype(jnp.bfloat16)
    )
    updated = (middle.astype(jnp.float32) + project_rows(cross_attended, w_cout)).astype(
        jnp.bfloat16
    )
    grad_cout = weight_product(cross_attended, cotangent_rows)
    d_cross = project_back(cotangent_rows, w_cout).astype(jnp.bfloat16)
    d_cross_probs = einsum_mixed("bihd,bthd->bhit", split_heads(d_cross, heads), cvalue_heads)
    d_cross_scores = (
        cross_probs
        * (d_cross_probs - jnp.sum(cross_probs * d_cross_probs, axis=-1, keepdims=True))
        * scale
    ).astype(jnp.bfloat16)
    d_cross_query = (
        einsum_mixed("bhit,bthd->bihd", d_cross_scores, ckey_heads)
        .reshape(block_count, row_count, width)
        .astype(jnp.bfloat16)
    )
    grad_cquery = weight_product(middle, d_cross_query)
    d_middle = (cotangent_rows.astype(jnp.float32) + project_back(d_cross_query, w_cquery)).astype(
        jnp.bfloat16
    )
    grad_out = weight_product(attended, d_middle)
    d_attended = project_back(d_middle, w_out).astype(jnp.bfloat16)
    dattn_heads = split_heads(d_attended, heads)
    d_probs = einsum_mixed("bihd,bjhd->bhij", dattn_heads, value_heads)
    d_scores = (
        probs * (d_probs - jnp.sum(probs * d_probs, axis=-1, keepdims=True)) * scale
    ).astype(jnp.bfloat16)
    d_query = (
        einsum_mixed("bhij,bjhd->bihd", d_scores, key_heads)
        .reshape(block_count, row_count, width)
        .astype(jnp.bfloat16)
    )
    d_key = (
        einsum_mixed("bhij,bihd->bjhd", d_scores, query_heads)
        .reshape(block_count, row_count, width)
        .astype(jnp.bfloat16)
    )
    d_value = (
        einsum_mixed("bhij,bihd->bjhd", probs_rounded, dattn_heads)
        .reshape(block_count, row_count, width)
        .astype(jnp.bfloat16)
    )
    grad_query = weight_product(block_atoms, d_query)
    grad_key = weight_product(block_atoms, d_key)
    grad_value = weight_product(block_atoms, d_value)
    grads = jnp.stack([grad_query, grad_key, grad_value, grad_out, grad_cquery, grad_cout])
    return (updated, grads)


def on_device(
    atoms,
    distance_bins,
    bonds,
    molecule,
    block_counts,
    block_scaffold,
    pocket_ids,
    pocket_keys,
    pocket_values,
    pocket_bias,
    bin_table,
    bond_weight,
    w_query,
    w_key,
    w_value,
    w_out,
    w_cross_query,
    w_cross_out,
    cotangent,
):
    dp_count = lax.axis_size("dp")
    pocket_count = lax.axis_size("pocket")
    capacity = atoms.shape[0]
    balanced = cotangent.shape[0]
    row_count = atoms.shape[1]
    width = atoms.shape[2]
    heads = bin_table.shape[0]
    per_target = capacity // dp_count
    counts = lax.all_gather(block_counts.reshape(1), "dp", axis=0, tiled=True)
    offsets = jnp.cumsum(counts) - counts
    own_device = lax.axis_index("dp")
    own_column = lax.axis_index("pocket")
    own_offset = offsets[own_device]
    own_count = counts[own_device]
    target_rows = lax.broadcasted_iota(jnp.int32, (dp_count, per_target), 0)
    turn_index = lax.broadcasted_iota(jnp.int32, (dp_count, per_target), 1)
    outgoing = jnp.mod(target_rows - own_offset, dp_count) + dp_count * turn_index
    picked = jnp.where(outgoing < own_count, outgoing, 0).reshape(-1)
    source_offset = offsets[:, None]
    source_count = counts[:, None]
    incoming = jnp.mod(own_device - source_offset, dp_count) + dp_count * turn_index
    usable = incoming < source_count
    landing = (source_offset + incoming) // dp_count
    wanted = lax.broadcasted_iota(jnp.int32, (balanced, 1), 0)
    matches = (landing.reshape(1, -1) == wanted) & usable.reshape(1, -1)
    received_index = lax.broadcasted_iota(jnp.int32, (balanced, dp_count * per_target), 1)
    position = jnp.sum(jnp.where(matches, received_index, 0), axis=1)
    local_bias = pair_bias(distance_bins, bonds, molecule, bin_table, bond_weight)
    got_atoms, got_bias = (
        lax.all_to_all(atoms[picked], "dp", split_axis=0, concat_axis=0, tiled=True),
        lax.all_to_all(local_bias[picked], "dp", split_axis=0, concat_axis=0, tiled=True),
    )
    block_atoms = got_atoms[position]
    block_bias = got_bias[position]
    anchor = ((target_rows * pocket_count + own_column) * capacity + incoming).reshape(-1)[position]
    scaffold = block_scaffold[anchor]
    all_keys, all_values, all_bias = (
        lax.all_gather(pocket_keys, "pocket", axis=0, tiled=True),
        lax.all_gather(pocket_values, "pocket", axis=0, tiled=True),
        lax.all_gather(pocket_bias, "pocket", axis=1, tiled=True),
    )
    pocket_blocks = all_keys.shape[0] // row_count
    chosen = pocket_ids[scaffold]
    cross_keys = all_keys.reshape(pocket_blocks, row_count, width)[chosen].reshape(
        balanced, -1, width
    )
    cross_values = all_values.reshape(pocket_blocks, row_count, width)[chosen].reshape(
        balanced, -1, width
    )
    cross_bias = jnp.transpose(
        all_bias.reshape(heads, pocket_blocks, row_count)[:, chosen], (1, 0, 2, 3)
    ).reshape(balanced, heads, -1)
    per_pass = math.gcd(balanced, max(1, 512 // row_count))
    passes = balanced // per_pass
    weights = (w_query, w_key, w_value, w_out, w_cross_query, w_cross_out)

    def regroup(matrix):
        return matrix.reshape((passes, per_pass) + matrix.shape[1:])

    def one_pass(total, inputs):
        pass_atoms, pass_bias, pass_keys, pass_values, pass_cross_bias, pass_cotangent = inputs
        updated_rows, grads = layer_pass(
            pass_atoms,
            pass_bias,
            pass_keys,
            pass_values,
            pass_cross_bias,
            pass_cotangent,
            weights,
            heads,
        )
        return (total + grads, updated_rows)

    start_total = jnp.zeros((6, width, width), jnp.float32)
    total, updated = lax.scan(
        one_pass,
        start_total,
        (
            regroup(block_atoms),
            regroup(block_bias),
            regroup(cross_keys),
            regroup(cross_values),
            regroup(cross_bias),
            regroup(cotangent),
        ),
    )
    updated = updated.reshape(cotangent.shape)
    scale = 1.0 / math.sqrt(balanced * row_count * dp_count * pocket_count)
    weight_grads = (lax.psum(total, ("dp", "pocket")) * scale).astype(jnp.bfloat16)
    return (updated, weight_grads)


def solution(mesh):
    return jax.shard_map(
        on_device,
        mesh=mesh,
        in_specs=(
            P(("dp", "pocket"), None, None),
            P(("dp", "pocket"), None, None),
            P(("dp", "pocket"), None, None),
            P(("dp", "pocket"), None),
            P("dp", "pocket"),
            P(),
            P(),
            P("pocket", None),
            P("pocket", None),
            P(None, "pocket"),
            P(),
            P(),
            P(),
            P(),
            P(),
            P(),
            P(),
            P(),
            P(("dp", "pocket"), None, None),
        ),
        out_specs=(P(("dp", "pocket"), None, None), P()),
        check_vma=False,
    )
```

profile of v0, /device:TPU:1, one launch (start us, length us, event | category | flops | bytes accessed | tf_op | source)
XLA Modules:
  0.0 476.7 jit_solution(13174254826781527233)
XLA Ops:
  11.2 10.9 %all-reduce = s32[8]{0:T(128)S(1)} all-reduce(s32[8]{0:T(128)S(1)} %bitcast_dynamic-update-slice_fusion.6), channel_id=2, replica_groups=mesh['dp'=8,'pocket'=16] {'dp'}, use_global_device_ids=true, to_apply=%add | all-reduce | flops 8 | bytes 64 | tf_op jit(solution)/shard_map/all_gather | solution.py:176
  23.2 1.3 gather_fusion.5
  27.0 1.8 gather_fusion
  28.8 3.7 all-to-all-start
  32.8 7.7 %fusion.8 = bf16[8,12,128,128]{3,1,2,0:T(8,128)(2,1)} fusion(f32[8,128,128]{2,1,0:T(8,128)S(1)} %convert_element_type.163, f32[12]{0:T(128)S(1)} %copy-done.27, pred[8,128,128]{2,1,0:T(8,128)(4,1)S(1)} %broadcast_compare_fusion, s32[8,128,128]{2,1,0:T(8,128)S(1)} %copy-done.25, f32[12,32]{1,0:T(8,128)S(1)} %copy-done.26), kind=kOutput, calls=%fused_computation.25 | convolution fusion | flops 614465536 | bytes 4326960 | tf_op jit(solution)/shard_map/cijn,hn->chij/dot_general | solution.py:15
  40.6 5.2 %gather_fusion.2 = bf16[8,12,128,128]{3,1,2,0:T(8,128)(2,1)} fusion(bf16[8,12,128,128]{3,1,2,0:T(8,128)(2,1)} %fusion.8, s32[1024]{0:T(1024)S(1)} %get-tuple-element.40), kind=kCustom, calls=%fused_computation.2 | custom fusion | bytes 6291488 | tf_op jit(solution)/shard_map/gather | solution.py:198
  45.8 4.9 %copy.147 = bf16[8,12,128,128]{3,2,1,0:T(8,128)(2,1)} copy(bf16[8,12,128,128]{3,1,2,0:T(8,128)(2,1)} %gather_fusion.2) | data formatting | bytes 6291456 | tf_op jit(solution)/shard_map/gather | solution.py:198
  52.0 4.4 all-to-all-start.1
  56.5 56.4 %all_gather.15 = bf16[12,2048]{1,0:T(8,128)(2,1)S(1)} all-gather(bf16[12,128]{1,0:T(8,128)(2,1)S(1)} %copy-done.22), channel_id=1, replica_groups=mesh['dp'=8,'pocket'=16] {'pocket'}, dimensions={1}, use_global_device_ids=true | all-gather | bytes 52224 | tf_op jit(solution)/shard_map/all_gather | solution.py:207
  112.9 2.8 convolution_convert_fusion.1
  115.7 2.3 copy.161
  118.0 2.7 copy.151
  120.7 2.8 gather_fusion.6
  124.9 2.1 convolution_convert_fusion.3
  130.2 2.0 convolution_convert_fusion.5
  132.6 3.0 gather_fusion.3
  135.7 1.6 copy.148
  137.3 4.8 %fusion.84 = (f32[4,12,128]{2,1,0:T(8,128)S(1)}, f32[4,12,128,128]{2,3,1,0:T(8,128)}) fusion(bf16[4,12,128,128]{2,3,1,0:T(8,128)(2,1)} %copy.148, bf16[4,128,12,64]{1,3,2,0:T(8,128)(2,1)} %bitcast.165, bf16[4,128,12,64]{1,3,2,0:T(8,128)(2,1)} %bitcast.163), kind=kOutput, calls=%fused_computation.129 | convolution fusion | flops 104595584 | bytes 6316032 | tf_op jit(solution)/shard_map/while/body/eval_jaxpr/sub | solution.py:48
  142.1 2.5 convolution_convert_fusion.7
  145.9 1.7 convolution_convert_fusion.2
  147.6 1.5 copy.153
  149.1 4.3 gather_fusion.8
  153.4 4.3 gather_fusion.7
  157.7 5.1 %copy.152 = bf16[16,128,768]{1,0,2:T(8,128)(2,1)} copy(bf16[16,128,768]{2,1,0:T(8,128)(2,1)} %gather_fusion.7) | data formatting | bytes 6291456 | tf_op jit(solution)/shard_map/gather | solution.py:214
  162.8 5.7 %reshape.368 = bf16[4,512,12,64]{1,0,3,2:T(4,128)(2,1)} reshape(bf16[16,128,768]{1,0,2:T(8,128)(2,1)} %copy.152) | data formatting | bytes 6291456 | tf_op jit(solution)/shard_map/while/body/eval_jaxpr/reshape | solution.py:53
  168.5 5.1 %copy.154 = bf16[16,128,768]{1,0,2:T(8,128)(2,1)} copy(bf16[16,128,768]{2,1,0:T(8,128)(2,1)} %gather_fusion.8) | data formatting | bytes 6291456 | tf_op jit(solution)/shard_map/gather | solution.py:211
  173.6 5.7 %reshape.371 = bf16[4,512,12,64]{1,0,3,2:T(4,128)(2,1)} reshape(bf16[16,128,768]{1,0,2:T(8,128)(2,1)} %copy.154) | data formatting | bytes 6291456 | tf_op jit(solution)/shard_map/while/body/eval_jaxpr/reshape | solution.py:53
  179.4 3.7 fusion.25
  183.1 6.6 %fusion.85 = (f32[4,12,128]{2,1,0:T(8,128)S(1)}, f32[4,12,128,512]{3,2,1,0:T(8,128)}) fusion(f32[4,12,128,512]{3,2,1,0:T(8,128)S(1)} %fusion.25, f32[4,12,512]{2,1,0:T(8,128)S(1)} %copy.158), kind=kOutput, calls=%fused_computation.130 | output fusion | flops 18874880 | bytes 25288704 | tf_op jit(solution)/shard_map/while/body/eval_jaxpr/sub | solution.py:48
  189.7 8.8 %fusion.21 = f32[4,12,128,512]{3,2,1,0:T(8,128)} fusion(bf16[4,128,12,64]{1,3,2,0:T(8,128)(2,1)S(1)} %bitcast.151, bf16[4,512,12,64]{1,0,3,2:T(4,128)(2,1)} %reshape.368), kind=kOutput, calls=%fused_computation.39 | convolution fusion | flops 402653184 | bytes 16515072 | tf_op jit(solution)/shard_map/while/body/eval_jaxpr/bihd,bthd->bhit/dot_general | solution.py:57
  198.5 5.4 %fusion.50 = bf16[4,12,64,128]{3,2,1,0:T(8,128)(2,1)} fusion(bf16[4,512,12,64]{1,0,3,2:T(4,128)(2,1)} %reshape.368, f32[4,12,128,512]{3,2,1,0:T(8,128)S(1)} %copy-done.2, f32[4,12,128]{2,1,0:T(8,128)S(1)} %get-tuple-element.37), kind=kOutput, calls=%fused_computation.70 | convolution fusion | flops 409337856 | bytes 16539648 | tf_op jit(solution)/shard_map/while/body/eval_jaxpr/bhit,bthd->bihd/dot_general | solution.py:57
  203.9 44.4 %fusion.39 = bf16[4,12,64,128]{3,2,1,0:T(8,128)(2,1)} fusion(f32[4,12,128,512]{3,2,1,0:T(8,128)} %fusion.21, bf16[4,512,12,64]{1,0,3,2:T(4,128)(2,1)} %reshape.371, f32[4,12,128,512]{3,2,1,0:T(8,128)} %get-tuple-element.38, f32[4,12,128]{2,1,0:T(8,128)S(1)} %get-tuple-element.37), kind=kOutput, calls=%fused_computation.61 | convolution fusion | flops 425073152 | bytes 29122560 | tf_op jit(solution)/shard_map/while/body/eval_jaxpr/bhit,bthd->bihd/dot_general | solution.py:57
  248.3 2.4 add_convert_fusion
  251.7 1.7 convolution_convert_fusion
  253.4 1.5 copy.165
  254.9 4.1 convolution_convert_fusion.6
  258.9 2.3 fusion.86
  261.2 6.9 %fusion.44 = bf16[4,12,64,128]{3,2,1,0:T(8,128)(2,1)} fusion(bf16[4,128,12,64]{1,3,2,0:T(8,128)(2,1)} %bitcast.164, f32[4,12,128,128]{2,3,1,0:T(8,128)} %fusion.86, f32[4,12,128,128]{2,3,1,0:T(8,128)} %get-tuple-element.36, f32[4,12,128]{2,1,0:T(8,128)S(1)} %get-tuple-element.35), kind=kOutput, calls=%fused_computation.68 | convolution fusion | flops 106567808 | bytes 7888896 | tf_op jit(solution)/shard_map/while/body/eval_jaxpr/bhij,bjhd->bihd/dot_general | solution.py:57
  268.1 6.6 %fusion.47 = bf16[4,12,64,128]{3,2,1,0:T(8,128)(2,1)} fusion(bf16[4,128,12,64]{1,3,2,0:T(8,128)(2,1)S(1)} %bitcast.166, f32[4,12,128,128]{2,3,1,0:T(8,128)} %fusion.86, f32[4,12,128,128]{2,3,1,0:T(8,128)} %get-tuple-element.36, f32[4,12,128]{2,1,0:T(8,128)S(1)} %get-tuple-element.35), kind=kOutput, calls=%fused_computation.69 | convolution fusion | flops 106567808 | bytes 7888896 | tf_op jit(solution)/shard_map/while/body/eval_jaxpr/bhij,bihd->bjhd/dot_general | solution.py:57
  274.7 3.5 bitcast_dynamic-update-slice_fusion.5
  278.2 2.2 bitcast_dynamic-update-slice_fusion.4
  280.4 2.3 bitcast_dynamic-update-slice_fusion.3
  282.7 2.2 bitcast_dynamic-update-slice_fusion.2
  285.0 2.2 bitcast_dynamic-update-slice_fusion.1
  287.2 2.3 bitcast_dynamic-update-slice_fusion
  290.7 1.7 add_convert_fusion.1
  292.4 168.1 %all-reduce.3.cloned.1.call-done = f32[6,768,768]{2,1,0:T(8,128)} async-done(((f32[6,768,768]{2,1,0:T(8,128)}), f32[6,768,768]{2,1,0:T(8,128)}) %all-reduce.3.cloned.1.call-update) | async-done | bytes 14155792 | tf_op jit(solution)/shard_map/psum | solution.py:256
  460.5 9.4 %multiply_convert_fusion = bf16[6,768,768]{2,1,0:T(8,128)(2,1)} fusion(f32[6,768,768]{2,1,0:T(8,128)} %all-reduce.3.cloned.1.call-done), kind=kLoop, calls=%fused_computation.16 | loop fusion | flops 7077888 | bytes 21233664 | tf_op jit(solution)/shard_map/convert_element_type | solution.py:256
  (102 shorter events, 16.9 us)
Async XLA Ops:
  7.2 19.8 %copy-start = (bf16[8,128,768]{2,1,0:T(8,128)(2,1)S(1)}, bf16[8,128,768]{2,1,0:T(8,128)(2,1)}, u32[]{:S(2)}) copy-start(bf16[8,128,768]{2,1,0:T(8,128)(2,1)} %param.19) | copy-start | bytes 4718596
  7.2 141.9 %all-gather.6.cloned.1.call-start = ((), (), s32[]{:S(2)}) async-start(), calls=%async_computation.3 | async-start | bytes 3342336 | tf_op jit(solution)/shard_map/all_gather | solution.py:205
  7.9 145.5 %all-gather.4.cloned.1.call-start = ((), (), s32[]{:S(2)}) async-start(), calls=%async_computation.2 | async-start | bytes 3342336 | tf_op jit(solution)/shard_map/all_gather | solution.py:206
  27.0 5.6 %copy-start.21 = (s32[8,128]{1,0:T(8,128)S(1)}, s32[8,128]{1,0:T(8,128)}, u32[]{:S(2)}) copy-start(s32[8,128]{1,0:T(8,128)} %param.22) | copy-start | bytes 12292
  27.0 5.8 %copy-start.26 = (f32[12,32]{1,0:T(8,128)S(1)}, f32[12,32]{1,0:T(8,128)}, u32[]{:S(2)}) copy-start(f32[12,32]{1,0:T(8,128)} %param.29) | copy-start | bytes 4612
  27.0 5.8 %copy-start.27 = (f32[12]{0:T(128)S(1)}, f32[12]{0:T(128)}, u32[]{:S(2)}) copy-start(f32[12]{0:T(128)} %param.30) | copy-start | bytes 148
  28.8 3.7 copy-start.19
  28.8 4.0 copy-start.25
  28.8 23.1 %all-to-all-start = ((bf16[8,128,768]{2,1,0:T(8,128)(2,1)}), bf16[8,128,768]{2,1,0:T(8,128)(2,1)S(1)}, u32[]{:S(2)}, u32[]{:S(2)}) async-start(bf16[8,128,768]{2,1,0:T(8,128)(2,1)} %gather_fusion), calls=%async_computation | async-start | bytes 3145728 | tf_op jit(solution)/shard_map/all_to_all | solution.py:197
  50.6 5.8 %copy-start.22 = (bf16[12,128]{1,0:T(8,128)(2,1)S(1)}, bf16[12,128]{1,0:T(8,128)(2,1)}, u32[]{:S(2)}) copy-start(bf16[12,128]{1,0:T(8,128)(2,1)} %param.28) | copy-start | bytes 9220
  50.6 62.3 %copy-start.9 = (bf16[768,768]{1,0:T(8,128)(2,1)S(1)}, bf16[768,768]{1,0:T(8,128)(2,1)}, u32[]{:S(2)}) copy-start(bf16[768,768]{1,0:T(8,128)(2,1)} %param.36) | copy-start | bytes 3538948
  52.0 80.7 %all-to-all-start.1 = ((bf16[8,12,128,128]{3,2,1,0:T(8,128)(2,1)}), bf16[8,12,128,128]{3,2,1,0:T(8,128)(2,1)}, u32[]{:S(2)}, u32[]{:S(2)}) async-start(bf16[8,12,128,128]{3,2,1,0:T(8,128)(2,1)} %copy.147), calls=%async_computation.1 | async-start | bytes 6291456 | tf_op jit(solution)/shard_map/all_to_all | solution.py:198
  56.4 61.6 %copy-start.20 = (s32[8192,4]{0,1:T(4,128)S(1)}, s32[8192,4]{0,1:T(4,128)}, u32[]{:S(2)}) copy-start(s32[8192,4]{0,1:T(4,128)} %param.25) | copy-start | bytes 393220
  56.4 404.1 %all-reduce.3.cloned.1.call-start = ((), (), s32[]{:S(2)}) async-start(), calls=%async_computation.4 | async-start | bytes 28311552 | tf_op jit(solution)/shard_map/psum | solution.py:256
  124.9 3.3 copy-start.23
  132.6 9.5 %copy-start.4 = (bf16[4,128,768]{1,2,0:T(8,128)(2,1)}, bf16[4,128,768]{1,2,0:T(8,128)(2,1)S(1)}, u32[]{:S(2)}) copy-start(bf16[4,128,768]{1,2,0:T(8,128)(2,1)S(1)} %copy.144) | copy-start | bytes 2359300
  142.1 2.6 copy-start.7
  144.6 1.3 copy-start.24
  183.1 6.6 %copy-start.3 = (bf16[4,128,768]{1,2,0:T(8,128)(2,1)S(1)}, bf16[4,128,768]{1,2,0:T(8,128)(2,1)}, u32[]{:S(2)}) copy-start(bf16[4,128,768]{1,2,0:T(8,128)(2,1)} %copy.161) | copy-start | bytes 2359300
  189.7 8.8 %copy-start.2 = (f32[4,12,128,512]{3,2,1,0:T(8,128)S(1)}, f32[4,12,128,512]{3,2,1,0:T(8,128)}, u32[]{:S(2)}) copy-start(f32[4,12,128,512]{3,2,1,0:T(8,128)} %get-tuple-element.38) | copy-start | bytes 37748740
  203.9 44.4 %copy-start.12 = (bf16[4,128,768]{2,1,0:T(8,128)(2,1)S(1)}, bf16[4,128,768]{2,1,0:T(8,128)(2,1)}, u32[]{:S(2)}) copy-start(bf16[4,128,768]{2,1,0:T(8,128)(2,1)} %param.37) | copy-start | bytes 2359300
  248.3 3.4 copy-start.8
  250.7 0.9 copy-start.15
  254.9 4.1 copy-start.5
  261.2 6.9 %copy-start.11 = (bf16[4,128,768]{1,2,0:T(8,128)(2,1)S(1)}, bf16[4,128,768]{1,2,0:T(8,128)(2,1)}, u32[]{:S(2)}) copy-start(bf16[4,128,768]{1,2,0:T(8,128)(2,1)} %copy.145) | copy-start | bytes 2359300
  274.7 3.5 copy-start.18
  274.7 5.7 %copy-start.17 = (bf16[4,12,64,128]{3,2,1,0:T(8,128)(2,1)S(1)}, bf16[4,12,64,128]{3,2,1,0:T(8,128)(2,1)}, u32[]{:S(2)}) copy-start(bf16[4,12,64,128]{3,2,1,0:T(8,128)(2,1)} %convolution_convert_fusion.6) | copy-start | bytes 2359300
  278.2 4.5 copy-start.16
  280.4 4.5 copy-start.14
  282.7 4.5 copy-start.6
  282.7 4.5 copy-start.13
  289.4 1.3 copy-start.10
  460.5 9.4 %copy-start.1 = (bf16[8,128,768]{2,1,0:T(8,128)(2,1)S(1)}, bf16[8,128,768]{2,1,0:T(8,128)(2,1)}, u32[]{:S(2)}) copy-start(bf16[8,128,768]{2,1,0:T(8,128)(2,1)} %param.19) | copy-start | bytes 4718596
Sparse Core Ops, SparseCore 0:
  10.4 61.3 all-gather.5
  74.1 51.4 all-gather.3
  289.6 170.8 all-reduce.2
where the time goes:
time: 483 us; the launch traced here: 477 us
  waiting for transfers between devices  171 us (35%)
  matrix products  128 us (27%)
  local copies, waits for them, and re-layouts  69.3 us (14%)
  blocking collectives  67.3 us (14%)
  other arithmetic  17.9 us (4%)
  between operations  15.1 us (3%)
  starting transfers between devices  8.27 us (2%)
    psum x1, waiting for transfers between devices, on_device(): lax.psum(total, ('dp', 'pocket')) * scale  168 us
    dot_general x9, matrix products, einsum_mixed(): return jnp.einsum(form, left, right, preferred_element_type=jnp.float32)  84.6 us
    all_gather x1, blocking collectives, on_device(): lax.all_gather(pocket_bias, 'pocket', axis=1, tiled=True)  56.4 us
    dot_general x6, matrix products, weight_product(): lax.dot_general(left.reshape(-1, left.shape[-1]), right.reshape(-1, right...  14.7 us
    reshape x2, local copies, waits for them, and re-layouts, split_heads(): matrix.reshape(matrix.shape[0], matrix.shape[1], heads, matrix.shape[2] /...  11.4 us
    all_gather x1, blocking collectives, on_device(): counts = lax.all_gather(block_counts.reshape(1), 'dp', axis=0, tiled=True)  10.9 us
    gather x2, local copies, waits for them, and re-layouts, on_device(): local_bias[picked]  10.1 us
  transfers between devices with their start and end apart: 5, of which 2 were waited for; matrix products, arithmetic and copies ran while one was open for 14% of the time, Pallas kernels for 0%

commit v1 on v0

v1 whole, which is shorter than its diff:
```python
import math

import jax
import jax.numpy as jnp
from jax import lax
from jax.experimental import pallas as pl
from jax.experimental.pallas import tpu as pltpu
from jax.sharding import Mesh
from jax.sharding import PartitionSpec as P

masked_value = -30000.0
f32, bf16 = jnp.float32, jnp.bfloat16
A, D, H = 128, 768, 12
PAIRS = 6
NB = 4
T = 512
HALF = D // 2


def mm(a, b):
    return lax.dot_general(a, b, (((1,), (0,)), ((), ())), preferred_element_type=f32)


def mm_t(a, b):
    return lax.dot_general(a, b, (((1,), (1,)), ((), ())), preferred_element_type=f32)


def mm_l(a, b):
    return lax.dot_general(a, b, (((0,), (0,)), ((), ())), preferred_element_type=f32)


def low_lanes():
    return lax.broadcasted_iota(jnp.int32, (A, A), 1) < A // 2


def stack_heads(pair, low):
    zero = jnp.zeros_like(pair)
    return jnp.concatenate([jnp.where(low, pair, zero), jnp.where(low, zero, pair)], axis=0)


def join_heads(both, low):
    return jnp.where(low, both[:A], both[A:])


def softmax(s):
    e = jnp.exp(s - jnp.max(s, axis=-1, keepdims=True))
    return e * pl.reciprocal(jnp.sum(e, axis=-1, keepdims=True))


def cols(p):
    return slice(p * A, (p + 1) * A)


def self_kernel(src, slot, got, mol, table, w_q, w_k, w_v, w_o, w_cq, w_co, cot,
                x_o, q_o, k_o, v_o, p_o, at_o, mid_o, cq_o, dc_o, buf, idx, sems):
    for b in range(NB):
        pltpu.make_async_copy(got.at[src[b]], buf.at[b], sems.at[b]).start()
    dc_o[...] = mm_t(cot[...], w_co[...]).astype(bf16)
    for b in range(NB):
        pltpu.make_async_copy(got.at[src[b]], buf.at[b], sems.at[b]).wait()
        rows = slice(b * A, (b + 1) * A)
        x_o[rows, :] = buf[b, :, :D]
        bins = buf[b, :, D:D + A].astype(f32).astype(jnp.int32)
        bond = buf[b, :, D + A:].astype(f32).astype(jnp.int32)
        own = jnp.broadcast_to(mol[pl.ds(src[b] * 8 + slot[b], 1), :].astype(f32), (A, A))
        idx[b] = jnp.where(own == own.T, bins + 32 * bond, 64)
    x = x_o[...]
    q_o[...] = mm(x, w_q[...]).astype(bf16) * 0.125
    k_o[...] = mm(x, w_k[...]).astype(bf16)
    v_o[...] = mm(x, w_v[...]).astype(bf16)
    low = low_lanes()

    def block(b, carry):
        rows = pl.ds(pl.multiple_of(b * A, A), A)
        codes = idx[b]
        for p in range(PAIRS):
            s = mm_t(stack_heads(q_o[rows, cols(p)], low), k_o[rows, cols(p)])
            bias = [
                jnp.take_along_axis(jnp.broadcast_to(table[2 * p + h:2 * p + h + 1, :], (A, A)), codes, axis=1)
                for h in range(2)
            ]
            probs = softmax(s + jnp.concatenate(bias, axis=0))
            p_o[b, p] = probs
            o = mm(probs.astype(bf16), v_o[rows, cols(p)])
            at_o[rows, cols(p)] = join_heads(o, low).astype(bf16)
        return carry

    lax.fori_loop(0, NB, block, 0)
    mid = (x.astype(f32) + mm(at_o[...], w_o[...])).astype(bf16)
    mid_o[...] = mid
    cq_o[...] = mm(mid, w_cq[...]).astype(bf16) * 0.125


def cross_kernel(chosen, me, *refs):
    near, far = refs[:8], refs[8:16]
    (cq, dc, mid, at, cot, w_co, w_cq, w_o, up_o, da_o, keep_o, send_o, pocket, ca, dcq, sems) = refs[16:]
    x, yh, c = me[0], me[1], me[2]

    def copies():
        out = []
        for i in range(8):
            group = ((x + 4 - i // 2) % 4) * 2 + (yh + i) % 2
            out.append(pltpu.make_async_copy(near[i], pocket.at[group * 2 + c], sems.at[i]))
            out.append(pltpu.make_async_copy(far[i], pocket.at[group * 2 + 1 - c], sems.at[8 + i]))
        return out

    for copy in copies():
        copy.start()
    low = low_lanes()
    for copy in copies():
        copy.wait()

    def block(b, carry):
        rows = pl.ds(pl.multiple_of(b * A, A), A)
        names = [chosen[b * 4 + t] for t in range(4)]
        for p in range(PAIRS):
            kk = jnp.concatenate([pocket[n, :A, cols(p)] for n in names], axis=0)
            vv = jnp.concatenate([pocket[n, :A, cols(PAIRS + p)] for n in names], axis=0)
            s = mm_t(stack_heads(cq[rows, cols(p)], low), kk)
            bb = [
                jnp.broadcast_to(
                    jnp.concatenate([pocket[n, A:A + 1, cols(2 * p + h)] for n in names], axis=1).astype(f32), (A, T))
                for h in range(2)
            ]
            probs = softmax(s + jnp.concatenate(bb, axis=0))
            o = mm(probs.astype(bf16), vv)
            ca[rows, cols(p)] = join_heads(o, low).astype(bf16)
            dp = mm_t(stack_heads(dc[rows, cols(p)], low), vv)
            delta = jnp.sum(probs * dp, axis=-1, keepdims=True)
            ds = (probs * (dp - delta)).astype(bf16)
            dcq[rows, cols(p)] = (join_heads(mm(ds, kk), low) * 0.125).astype(bf16)
        return carry

    lax.fori_loop(0, NB, block, 0)
    up_o[...] = (mid[...].astype(f32) + mm(ca[...], w_co[...])).astype(bf16)
    dm = (cot[...].astype(f32) + mm_t(dcq[...], w_cq[...])).astype(bf16)
    da_o[...] = mm_t(dm, w_o[...]).astype(bf16)
    split_store(keep_o, send_o, 0, mm_l(at[...], dm).astype(bf16), c)
    split_store(keep_o, send_o, 1, mm_l(mid[...], dcq[...]).astype(bf16), c)
    split_store(keep_o, send_o, 2, mm_l(ca[...], cot[...]).astype(bf16), c)


def split_store(keep_o, send_o, i, full, c):
    lo, hi = full[:, :HALF], full[:, HALF:]

    @pl.when(c == 0)
    def _():
        keep_o[i] = lo
        send_o[i] = hi

    @pl.when(c == 1)
    def _():
        keep_o[i] = hi
        send_o[i] = lo


def back_kernel(me, x, q, k, v, probs, da, keep_o, send_o, dqkv):
    low = low_lanes()

    def block(b, carry):
        rows = pl.ds(pl.multiple_of(b * A, A), A)
        for p in range(PAIRS):
            dd = stack_heads(da[rows, cols(p)], low)
            dp = mm_t(dd, v[rows, cols(p)])
            pr = probs[b, p]
            delta = jnp.sum(pr * dp, axis=-1, keepdims=True)
            ds = (pr * (dp - delta)).astype(bf16)
            dqkv[rows, cols(p)] = (join_heads(mm(ds, k[rows, cols(p)]), low) * 0.125).astype(bf16)
            dqkv[rows, cols(6 + p)] = mm_l(ds, stack_heads(q[rows, cols(p)], low)).astype(bf16)
            dqkv[rows, cols(12 + p)] = mm_l(pr.astype(bf16), dd).astype(bf16)
        return carry

    lax.fori_loop(0, NB, block, 0)
    for i in range(3):
        split_store(keep_o, send_o, i, mm_l(x[...], dqkv[:, i * D:(i + 1) * D]).astype(bf16), me[2])


V = pl.BlockSpec(memory_space=pltpu.VMEM)
S = pl.BlockSpec(memory_space=pltpu.SMEM)
ANY = pl.BlockSpec(memory_space=pl.ANY)
R = NB * A


def sds(shape, dt=bf16):
    return jax.ShapeDtypeStruct(shape, dt)


def self_call(src, slot, got, mol, table, ws, cot):
    return pl.pallas_call(
        self_kernel,
        out_shape=[sds((R, D)) for _ in range(4)] + [sds((NB, PAIRS, 2 * A, A), f32)] + [sds((R, D)) for _ in range(4)],
        in_specs=[S, S, ANY] + [V] * 9,
        out_specs=[V] * 9,
        scratch_shapes=[pltpu.VMEM((NB, A, D + 2 * A), bf16), pltpu.VMEM((NB, A, A), jnp.int32),
                        pltpu.SemaphoreType.DMA((NB,))],
        name="self_forward",
    )(src, slot, got, mol, table, *ws, cot)


def cross_call(chosen, me, near, far, cq, dc, mid, at, cot, w_co, w_cq, w_o):
    return pl.pallas_call(
        cross_kernel,
        out_shape=[sds((R, D)), sds((R, D)), sds((3, D, HALF)), sds((3, D, HALF))],
        in_specs=[S, S] + [ANY] * 16 + [V] * 8,
        out_specs=[V] * 4,
        scratch_shapes=[pltpu.VMEM((16, A + 8, 2 * D), bf16), pltpu.VMEM((R, D), bf16), pltpu.VMEM((R, D), bf16),
                        pltpu.SemaphoreType.DMA((16,))],
        name="cross_both",
    )(chosen, me, *near, *far, cq, dc, mid, at, cot, w_co, w_cq, w_o)


def back_call(me, x, q, k, v, probs, da):
    return pl.pallas_call(
        back_kernel,
        out_shape=[sds((3, D, HALF)), sds((3, D, HALF))],
        in_specs=[S] + [V] * 6,
        out_specs=[V] * 2,
        scratch_shapes=[pltpu.VMEM((R, 3 * D), bf16)],
        name="self_backward",
    )(me, x, q, k, v, probs, da)


def pack_kernel(counts, me, atoms, bins, bonds, out):
    out[0, :, :D] = atoms[0]
    out[0, :, D:D + A] = bins[0].astype(f32).astype(bf16)
    out[0, :, D + A:] = bonds[0].astype(f32).astype(bf16)


def pack_call(counts, me, atoms, bins, bonds):
    def slot(t, counts, me):
        offset = sum(jnp.where(d < me[3], counts[d], 0) for d in range(8))
        return (t + 64 - offset) % 8, 0, 0

    return pl.pallas_call(
        pack_kernel,
        out_shape=sds((8, A, D + 2 * A)),
        grid_spec=pltpu.PrefetchScalarGridSpec(
            num_scalar_prefetch=2,
            grid=(8,),
            in_specs=[pl.BlockSpec((1, A, D), slot), pl.BlockSpec((1, A, A), slot), pl.BlockSpec((1, A, A), slot)],
            out_specs=pl.BlockSpec((1, A, D + 2 * A), lambda t, counts, me: (t, 0, 0)),
        ),
        name="pack_slots",
    )(counts, me, atoms, bins, bonds)


def index_kernel(counts, me, scaffold, ids, src_o, slot_o, chosen_o):
    dp, column = me[3], me[4]
    for b in range(NB):
        rank = b * 8 + dp
        source, begin, end = 0, 0, 0
        for d in range(8):
            end = end + counts[d]
            passed = (end <= rank).astype(jnp.int32)
            source = source + passed
            begin = jnp.where(passed == 1, end, begin)
        src_o[b] = source
        slot_o[b] = rank - begin
        name = scaffold[(source * 16 + column) * 8 + rank - begin]
        for t in range(4):
            chosen_o[b * 4 + t] = ids[t, name]


def index_call(counts, me, scaffold, ids):
    i32 = jnp.int32
    return pl.pallas_call(
        index_kernel,
        out_shape=[sds((NB,), i32), sds((NB,), i32), sds((NB * 4,), i32)],
        in_specs=[S] * 4,
        out_specs=[S] * 3,
        name="find_blocks",
    )(counts, me, scaffold, ids)


CHIPS = ("z", "yl", "x", "yh")


def exchange(matrix, axes):
    return lax.all_to_all(matrix, axes, split_axis=0, concat_axis=0, tiled=True)


def shifted(matrix, dx, dy):
    pairs = []
    for x in range(4):
        for y in range(2):
            pairs.append((x * 2 + y, (x + dx) % 4 * 2 + (y + dy) % 2))
    return lax.ppermute(matrix, ("x", "yh"), pairs)


def swap_core(matrix):
    return lax.ppermute(matrix, "c", [(0, 1), (1, 0)])


def reduce_grads(keep, send):
    half = (keep.astype(f32) + swap_core(send).astype(f32)).astype(bf16)
    pieces = exchange(half.reshape(64, -1, HALF), CHIPS)
    total = (jnp.sum(pieces.astype(f32), axis=0) * (1.0 / 256.0)).astype(bf16)
    return exchange(jnp.broadcast_to(total[None], pieces.shape), CHIPS).reshape(-1, D, HALF)


def on_device(
    atoms, distance_bins, bonds, molecule, block_counts, block_scaffold, pocket_ids, pocket_keys, pocket_values,
    pocket_bias, bin_table, bond_weight, w_query, w_key, w_value, w_out, w_cross_query, w_cross_out, cotangent,
):
    z, yl, x, yh, c = (lax.axis_index(n) for n in ("z", "yl", "x", "yh", "c"))
    me = jnp.stack([x, yh, c, z * 2 + yl, x * 4 + yh * 2 + c]).astype(jnp.int32)
    note = jnp.concatenate([molecule, jnp.broadcast_to(block_counts, (8, A))], axis=0)
    notes = exchange(jnp.broadcast_to(note[None], (8, 16, A)), ("z", "yl"))
    counts = notes[:, 8, 0]
    mol = notes[:, :8].reshape(64, A)
    got = exchange(pack_call(counts, me, atoms, distance_bins, bonds), ("z", "yl"))
    pocket = jnp.concatenate(
        [
            jnp.concatenate([pocket_keys, pocket_values], axis=1),
            jnp.broadcast_to(pocket_bias.reshape(1, 2 * D), (8, 2 * D)),
        ],
        axis=0,
    )
    near = [pocket if i == 0 else shifted(pocket, i // 2, i % 2) for i in range(8)]
    far = [swap_core(n) for n in near]
    src, slot, chosen = index_call(counts, me, block_scaffold, pocket_ids.T)
    table = jnp.concatenate(
        [
            bin_table,
            bin_table + bond_weight[:, None],
            jnp.full((H, A - 64), masked_value, f32),
        ],
        axis=1,
    )
    table = lax.reduce_precision(table, 8, 7)
    cot = cotangent.reshape(R, D)
    ws = (w_query, w_key, w_value, w_out, w_cross_query, w_cross_out)
    xs, q, k, v, probs, at, mid, cq, dc = self_call(src, slot, got, mol, table, ws, cot)
    updated, da, keep_a, send_a = cross_call(
        chosen, me, near, far, cq, dc, mid, at, cot, w_cross_out, w_cross_query, w_out
    )
    keep_b, send_b = back_call(me, xs, q, k, v, probs, da)
    mine = reduce_grads(jnp.concatenate([keep_b, keep_a]), jnp.concatenate([send_b, send_a]))
    theirs = swap_core(mine)
    low = jnp.where(c == 0, mine, theirs)
    high = jnp.where(c == 0, theirs, mine)
    return updated.reshape(cotangent.shape), jnp.concatenate([low, high], axis=2)


def solution(mesh):
    fine = Mesh(mesh.devices.reshape(4, 2, 4, 2, 2), ("z", "yl", "x", "yh", "c"))
    every = ("z", "yl", "x", "yh", "c")
    pocket = ("x", "yh", "c")
    return jax.shard_map(
        on_device,
        mesh=fine,
        in_specs=(
            P(every, None, None),
            P(every, None, None),
            P(every, None, None),
            P(every, None),
            P(("z", "yl"), pocket),
            P(),
            P(),
            P(pocket, None),
            P(pocket, None),
            P(None, pocket),
            P(),
            P(),
            P(),
            P(),
            P(),
            P(),
            P(),
            P(),
            P(every, None, None),
        ),
        out_specs=(P(every, None, None), P()),
        check_vma=False,
    )
```

time: 483 us -> 292 us (0.60); the launches traced: 477 us -> 291 us
  matrix products: 128 us -> 0 us
  waiting for transfers between devices: 171 us -> 51.6 us
  Pallas kernels: 0 us -> 73.8 us
  local copies, waits for them, and re-layouts: 69.3 us -> 6.44 us
  blocking collectives: 67.3 us -> 101 us
  starting transfers between devices: 8.27 us -> 41.3 us
  between operations: 15.1 us -> 1.5 us
    psum x1 -> x0, waiting for transfers between devices: 168 us -> none  [on_device(): lax.psum(total, ('dp', 'pocket')) * scale]
    dot_general x25 -> x0, matrix products: 123 us -> none  [the longest x9 84.6 us: einsum_mixed(): return jnp.einsum(form, left, right, preferred_element_type=jnp.float32)]
    all_to_all x0 -> x2, blocking collectives: none -> 101 us  [exchange(): return lax.all_to_all(matrix, axes, split_axis=0, concat_axis=0, tiled=True)]
    pallas_call x0 -> x5, Pallas kernels: none -> 73.8 us  [the longest x1 31.9 us: cross_call(): pl.pallas_call(cross_kernel, out_shape=[sds((R, D)), sds((R, D)), sds((3,...]
    all_gather x2 -> x0, blocking collectives: 67.3 us -> none  [the longest x1 56.4 us: on_device(): lax.all_gather(pocket_bias, 'pocket', axis=1, tiled=True)]
    ppermute x0 -> x17, waiting for transfers between devices: none -> 47.1 us  [the longest x7 34.9 us: shifted(): return lax.ppermute(matrix, ('x', 'yh'), pairs)]
    gather x14 -> x0, local copies, waits for them, and re-layouts: 41.2 us -> none  [the longest x2 10.1 us: on_device(): local_bias[picked]]
    ppermute x0 -> x17, starting transfers between devices: none -> 30.7 us  [the longest x10 17.7 us: swap_core(): return lax.ppermute(matrix, 'c', [(0, 1), (1, 0)])]
  transfers between devices with their start and end apart: 5 -> 19, of which waited for: 2 -> 8; matrix products, arithmetic and copies ran while one was open for 14% -> 1% of each run, Pallas kernels for 0% -> 7%
where the time goes in v1:
time: 292 us; the launch traced here: 291 us
  blocking collectives  101 us (35%)
  Pallas kernels  73.8 us (25%)
  waiting for transfers between devices  51.6 us (18%)
  starting transfers between devices  41.3 us (14%)
  other arithmetic  15.4 us (5%)
  local copies, waits for them, and re-layouts  6.44 us (2%)
    all_to_all x2, blocking collectives, exchange(): return lax.all_to_all(matrix, axes, split_axis=0, concat_axis=0, tiled=True)  101 us
    ppermute x7, waiting for transfers between devices, shifted(): return lax.ppermute(matrix, ('x', 'yh'), pairs)  34.9 us
    pallas_call x1, Pallas kernels, cross_call(): pl.pallas_call(cross_kernel, out_shape=[sds((R, D)), sds((R, D)), sds((3,...  31.9 us
    ppermute x10, starting transfers between devices, swap_core(): return lax.ppermute(matrix, 'c', [(0, 1), (1, 0)])  17.7 us
    pallas_call x1, Pallas kernels, back_call(): pl.pallas_call(back_kernel, out_shape=[sds((3, D, HALF)), sds((3, D, HALF...  16.2 us
    pallas_call x1, Pallas kernels, self_call(): pl.pallas_call(self_kernel, out_shape=[sds((R, D)) for _ in range(4)] + [...  15.5 us
    ppermute x7, starting transfers between devices, shifted(): return lax.ppermute(matrix, ('x', 'yh'), pairs)  13 us
    ppermute x10, waiting for transfers between devices, swap_core(): return lax.ppermute(matrix, 'c', [(0, 1), (1, 0)])  12.2 us
  transfers between devices with their start and end apart: 19, of which 8 were waited for; matrix products, arithmetic and copies ran while one was open for 1% of the time, Pallas kernels for 7%

profile of v1, /device:TPU:1, one launch (start us, length us, event | category | flops | bytes accessed | tf_op | source)
XLA Modules:
  0.0 290.9 jit_solution(11753369072922849718)
XLA Ops:
  1.3 0.7 concatenate.21
  2.0 0.6 broadcast_in_dim.13
  2.6 6.9 %all-to-all-start = ((s32[8,16,128]{2,1,0:T(8,128)}), s32[8,16,128]{2,1,0:T(8,128)S(1)}, u32[]{:S(2)}, u32[]{:S(2)}) async-start(s32[8,16,128]{2,1,0:T(8,128)} %broadcast_in_dim.13), calls=%async_computation | async-start | bytes 131072 | tf_op jit(solution)/shard_map/all_to_all | solution.py:279
  9.5 0.7 stack.23.me
  10.1 4.5 %all-to-all-done = s32[8,16,128]{2,1,0:T(8,128)S(1)} async-done(((s32[8,16,128]{2,1,0:T(8,128)}), s32[8,16,128]{2,1,0:T(8,128)S(1)}, u32[]{:S(2)}, u32[]{:S(2)}) %all-to-all-start) | async-done | bytes 65568 | tf_op jit(solution)/shard_map/all_to_all | solution.py:279
  14.7 0.8 slice_reduce_fusion.counts
  15.4 6.6 %pack_slots.1 = bf16[8,128,1024]{2,1,0:T(8,128)(2,1)} custom-call(s32[8]{0:T(128)} %slice_reduce_fusion.counts, s32[5]{0:T(128)} %stack.23.me, bf16[8,128,768]{2,1,0:T(8,128)(2,1)} %atoms.1, s32[8,128,128]{2,1,0:T(8,128)} %bins.1, s32[8,128,128]{2,1,0:T(8,128)} %bonds.1), custom_call_target="tpu_custom_call" | custom-call | tf_op jit(solution)/shard_map/pack_slots/pallas_call | solution.py:234
  22.1 3.7 %all-to-all-start.1 = ((bf16[8,128,1024]{2,1,0:T(8,128)(2,1)}), bf16[8,128,1024]{2,1,0:T(8,128)(2,1)S(1)}, u32[]{:S(2)}, u32[]{:S(2)}) async-start(bf16[8,128,1024]{2,1,0:T(8,128)(2,1)} %pack_slots.1), calls=%async_computation.1 | async-start | bytes 4194304 | tf_op jit(solution)/shard_map/all_to_all | solution.py:279
  25.9 2.2 collective-permute-start.7
  28.1 4.8 %collective-permute-start.6 = (bf16[136,1536]{1,0:T(8,128)(2,1)S(1)}, bf16[136,1536]{1,0:T(8,128)(2,1)S(1)}, u32[]{:S(2)}, u32[]{:S(2)}) collective-permute-start(bf16[136,1536]{1,0:T(8,128)(2,1)S(1)} %pad_maximum_fusion.2.refs_0_), channel_id=1, source_target_pairs={{0,14},{2,12},{4,2},{6,0},{8,6},{10,4},{12,10},{14,8},{1,15},{3,13... | collective-permute-start | bytes 1253384 | tf_op jit(solution)/shard_map/ppermute | solution.py:287
  32.9 0.5 collective-permute-start.5
  33.5 0.3 collective-permute-start.4
  33.8 2.7 collective-permute-start.3
  36.5 3.3 %collective-permute-start.2 = (bf16[136,1536]{1,0:T(8,128)(2,1)S(1)}, bf16[136,1536]{1,0:T(8,128)(2,1)}, u32[]{:S(2)}, u32[]{:S(2)}) collective-permute-start(bf16[136,1536]{1,0:T(8,128)(2,1)S(1)} %pad_maximum_fusion.2.refs_0_), channel_id=1, source_target_pairs={{0,6},{2,4},{4,10},{6,8},{8,14},{10,12},{12,2},{14,0},{1,7},{3,5},... | collective-permute-start | bytes 1253384 | tf_op jit(solution)/shard_map/ppermute | solution.py:287
  39.8 3.9 %collective-permute-done.6.refs_7_ = bf16[136,1536]{1,0:T(8,128)(2,1)S(1)} collective-permute-done((bf16[136,1536]{1,0:T(8,128)(2,1)S(1)}, bf16[136,1536]{1,0:T(8,128)(2,1)S(1)}, u32[]{:S(2)}, u32[]{:S(2)}) %collective-permute-start.6) | collective-permute-done | bytes 417824 | tf_op jit(solution)/shard_map/ppermute | solution.py:287
  43.6 1.4 collective-permute-start.1
  45.0 10.5 %collective-permute-done.5.refs_6_ = bf16[136,1536]{1,0:T(8,128)(2,1)S(1)} collective-permute-done((bf16[136,1536]{1,0:T(8,128)(2,1)S(1)}, bf16[136,1536]{1,0:T(8,128)(2,1)S(1)}, u32[]{:S(2)}, u32[]{:S(2)}) %collective-permute-start.5) | collective-permute-done | bytes 417824 | tf_op jit(solution)/shard_map/ppermute | solution.py:287
  55.5 4.4 %collective-permute-start.14 = (bf16[136,1536]{1,0:T(8,128)(2,1)S(1)}, bf16[136,1536]{1,0:T(8,128)(2,1)S(1)}, u32[]{:S(2)}, u32[]{:S(2)}) collective-permute-start(bf16[136,1536]{1,0:T(8,128)(2,1)S(1)} %collective-permute-done.6.refs_7_), channel_id=1, source_target_pairs={{0,1},{1,0},{2,3},{3,2},{4,5},{5,4},{6,7},{7,6},{8,9},{9,8},{10,11... | collective-permute-start | bytes 1253384 | tf_op jit(solution)/shard_map/ppermute | solution.py:291
  59.9 0.6 collective-permute-done.3.refs_4_
  60.5 2.6 collective-permute-start.13
  63.3 13.6 %collective-permute-done.2.refs_3_ = bf16[136,1536]{1,0:T(8,128)(2,1)} collective-permute-done((bf16[136,1536]{1,0:T(8,128)(2,1)S(1)}, bf16[136,1536]{1,0:T(8,128)(2,1)}, u32[]{:S(2)}, u32[]{:S(2)}) %collective-permute-start.2) | collective-permute-done | bytes 417824 | tf_op jit(solution)/shard_map/ppermute | solution.py:287
  76.8 2.7 collective-permute-start.12
  79.5 6.4 %collective-permute-done.1.refs_2_ = bf16[136,1536]{1,0:T(8,128)(2,1)} collective-permute-done((bf16[136,1536]{1,0:T(8,128)(2,1)S(1)}, bf16[136,1536]{1,0:T(8,128)(2,1)}, u32[]{:S(2)}, u32[]{:S(2)}) %collective-permute-start.1) | collective-permute-done | bytes 417824 | tf_op jit(solution)/shard_map/ppermute | solution.py:287
  85.9 1.5 collective-permute-start.11
  87.4 1.3 collective-permute-start.10
  88.7 0.1 collective-permute-start.9
  88.8 0.7 copy-done.9
  89.4 0.1 collective-permute-start.8
  89.5 0.7 copy-done.10
  90.2 0.7 maximum_reduce-precision_fusion.table
  90.9 3.5 %find_blocks.1 = (s32[4]{0:T(128)}, s32[4]{0:T(128)}, s32[16]{0:T(128)}) custom-call(s32[8]{0:T(128)} %slice_reduce_fusion.counts, s32[5]{0:T(128)} %stack.23.me, s32[1024]{0:T(1024)} %scaffold.1, s32[4,8192]{1,0:T(4,128)} %bitcast.20), custom_call_target="tpu_custom_call" | custom-call | tf_op jit(solution)/shard_map/find_blocks/pallas_call | solution.py:266
  94.4 0.6 slice_bitcast_fusion.mol
  95.0 1.3 copy-done.1
  96.3 15.5 %self_forward.1 = (bf16[512,768]{1,0:T(8,128)(2,1)}, bf16[512,768]{1,0:T(8,128)(2,1)}, bf16[512,768]{1,0:T(8,128)(2,1)}, bf16[512,768]{1,0:T(8,128)(2,1)}, f32[4...) custom-call(s32[4]{0:T(128)} %get-tuple-element.21.src, ...), custom_call_target="tpu_custom_call" | custom-call | tf_op jit(solution)/shard_map/self_forward/pallas_call | solution.py:189
  111.9 31.9 %cross_both.1 = (bf16[512,768]{1,0:T(8,128)(2,1)}, bf16[512,768]{1,0:T(8,128)(2,1)}, bf16[3,768,384]{2,1,0:T(8,128)(2,1)}, bf16[3,768,384]{2,1,0:T(8,128)(2,1)}) custom-call(s32[16]{0:T(128)} %get-tuple-element.20.chosen, s32[5]{0:T(128)} %stack.23.me, bf16[136,1536]{1,0:T(8,128)(2,1)} %copy-done.5, bf16[136,1536]{1,0:T(8,128)(2,1)} %collective-permute-done.refs_1_, ...), custom_call_target="tpu_custom_call" | custom-call | tf_op jit(solution)/shard_map/cross_both/pallas_call | solution.py:201
  143.8 16.2 %self_backward.1 = (bf16[3,768,384]{2,1,0:T(8,128)(2,1)}, bf16[3,768,384]{2,1,0:T(8,128)(2,1)}) custom-call(s32[5]{0:T(128)} %stack.23.me, bf16[512,768]{1,0:T(8,128)(2,1)} %get-tuple-element.28.x, bf16[512,768]{1,0:T(8,128)(2,1)} %get-tuple-element.29.q, bf16[512,768]{1,0:T(8,128)(2,1)} %get-tuple-element.30.k, bf16[512,768]{1,0:T(8,128)(2,1)} %get-tuple-element.31.v, ...), custom_call_target="tpu_custom_call" | custom-call | tf_op jit(solution)/shard_map/self_backward/pallas_call | solution.py:213
  160.0 2.0 pad_maximum_fusion.1
  162.1 0.1 collective-permute-start.15
  162.1 6.2 %collective-permute-done.15 = bf16[6,768,384]{2,1,0:T(8,128)(2,1)S(1)} collective-permute-done((bf16[6,768,384]{2,1,0:T(8,128)(2,1)S(1)}, bf16[6,768,384]{2,1,0:T(8,128)(2,1)S(1)}, u32[]{:S(2)}, u32[]{:S(2)}) %collective-permute-start.15) | collective-permute-done | bytes 3538976 | tf_op jit(solution)/shard_map/ppermute | solution.py:291
  168.4 1.0 add_convert_fusion
  169.3 52.7 %all_to_all.20 = bf16[64,72,384]{2,1,0:T(8,128)(2,1)S(1)} all-to-all(bf16[64,72,384]{2,1,0:T(8,128)(2,1)S(1)} %bitcast.17), channel_id=1, replica_groups=mesh['z'=4,'yl'=2,'x'=4,'yh'=2,'c'=2] {'z','yl','x','yh'}, dimensions={0} | all-to-all | bytes 7077888 | tf_op jit(solution)/shard_map/all_to_all | solution.py:279
  222.0 0.5 convert_reduce_fusion
  222.5 0.3 broadcast_in_dim.33
  222.8 48.2 %all_to_all.21 = bf16[64,72,384]{2,1,0:T(8,128)(2,1)S(1)} all-to-all(bf16[64,72,384]{2,1,0:T(8,128)(2,1)S(1)} %broadcast_in_dim.33), channel_id=1, replica_groups=mesh['z'=4,'yl'=2,'x'=4,'yh'=2,'c'=2] {'z','yl','x','yh'}, dimensions={0} | all-to-all | bytes 7077888 | tf_op jit(solution)/shard_map/all_to_all | solution.py:279
  271.1 2.8 collective-permute-start.16
  273.9 6.0 %collective-permute-done.16 = bf16[6,768,384]{2,1,0:T(8,128)(2,1)} collective-permute-done((bf16[6,768,384]{2,1,0:T(8,128)(2,1)S(1)}, bf16[6,768,384]{2,1,0:T(8,128)(2,1)}, u32[]{:S(2)}, u32[]{:S(2)}) %collective-permute-start.16) | collective-permute-done | bytes 3538976 | tf_op jit(solution)/shard_map/ppermute | solution.py:291
  279.8 5.5 %broadcast_select_fusion.1 = (bf16[6,768,384]{2,1,0:T(8,128)(2,1)S(1)}, bf16[6,768,384]{2,1,0:T(8,128)(2,1)}) fusion(bf16[6,768,384]{2,1,0:T(8,128)(2,1)} %bitcast.16, bf16[6,768,384]{2,1,0:T(8,128)(2,1)} %collective-permute-done.16, pred[]{:T(512)S(6)} %eq.4), kind=kLoop, calls=%fused_computation.5 | loop fusion | flops 3538944 | bytes 14155777 | tf_op jit(solution)/shard_map/jit(_where)/select_n | solution.py:340
  285.4 5.6 %pad_maximum_fusion = bf16[6,768,768]{2,1,0:T(8,128)(2,1)} fusion(bf16[6,768,384]{2,1,0:T(8,128)(2,1)} %get-tuple-element.39, bf16[6,768,384]{2,1,0:T(8,128)(2,1)S(1)} %get-tuple-element.38), kind=kLoop, calls=%fused_computation | loop fusion | flops 14155776 | bytes 14155776 | tf_op jit(solution)/shard_map/concatenate | solution.py:342
  (47 shorter events, 0.3 us)
Async XLA Ops:
  2.6 12.1 %all-to-all-start = ((s32[8,16,128]{2,1,0:T(8,128)}), s32[8,16,128]{2,1,0:T(8,128)S(1)}, u32[]{:S(2)}, u32[]{:S(2)}) async-start(s32[8,16,128]{2,1,0:T(8,128)} %broadcast_in_dim.13), calls=%async_computation | async-start | bytes 131072 | tf_op jit(solution)/shard_map/all_to_all | solution.py:279
  15.4 10.4 %copy-start.14 = (bf16[12,128]{1,0:T(8,128)(2,1)S(1)}, bf16[12,128]{1,0:T(8,128)(2,1)}, u32[]{:S(2)}) copy-start(bf16[12,128]{1,0:T(8,128)(2,1)} %param.28) | copy-start | bytes 9220
  15.4 10.4 %copy-start.11 = (bf16[128,768]{1,0:T(8,128)(2,1)S(1)}, bf16[128,768]{1,0:T(8,128)(2,1)}, u32[]{:S(2)}) copy-start(bf16[128,768]{1,0:T(8,128)(2,1)} %param.27) | copy-start | bytes 589828
  15.4 10.4 %copy-start.12 = (bf16[128,768]{1,0:T(8,128)(2,1)S(1)}, bf16[128,768]{1,0:T(8,128)(2,1)}, u32[]{:S(2)}) copy-start(bf16[128,768]{1,0:T(8,128)(2,1)} %param.26) | copy-start | bytes 589828
  22.1 41.1 %copy-start.13 = (f32[12,32]{1,0:T(8,128)S(1)}, f32[12,32]{1,0:T(8,128)}, u32[]{:S(2)}) copy-start(f32[12,32]{1,0:T(8,128)} %param.29) | copy-start | bytes 4612
  22.1 41.1 %copy-start.15 = (f32[12]{0:T(128)S(1)}, f32[12]{0:T(128)}, u32[]{:S(2)}) copy-start(f32[12]{0:T(128)} %param.30) | copy-start | bytes 148
  22.1 72.9 %all-to-all-start.1 = ((bf16[8,128,1024]{2,1,0:T(8,128)(2,1)}), bf16[8,128,1024]{2,1,0:T(8,128)(2,1)S(1)}, u32[]{:S(2)}, u32[]{:S(2)}) async-start(bf16[8,128,1024]{2,1,0:T(8,128)(2,1)} %pack_slots.1), calls=%async_computation.1 | async-start | bytes 4194304 | tf_op jit(solution)/shard_map/all_to_all | solution.py:279
  25.9 86.0 %copy-start.5 = (bf16[136,1536]{1,0:T(8,128)(2,1)}, bf16[136,1536]{1,0:T(8,128)(2,1)S(1)}, u32[]{:S(2)}) copy-start(bf16[136,1536]{1,0:T(8,128)(2,1)S(1)} %pad_maximum_fusion.2.refs_0_) | copy-start | bytes 1253380
  25.9 10.6 %collective-permute-start.7 = (bf16[136,1536]{1,0:T(8,128)(2,1)S(1)}, bf16[136,1536]{1,0:T(8,128)(2,1)S(1)}, u32[]{:S(2)}, u32[]{:S(2)}) collective-permute-start(bf16[136,1536]{1,0:T(8,128)(2,1)S(1)} %pad_maximum_fusion.2.refs_0_), channel_id=1, source_target_pairs={{0,1},{1,0},{2,3},{3,2},{4,5},{5,4},{6,7},{7,6},{8,9},{9,8},{10,11... | collective-permute-start | bytes 1253384 | tf_op jit(solution)/shard_map/ppermute | solution.py:291
  28.1 15.5 %collective-permute-start.6 = (bf16[136,1536]{1,0:T(8,128)(2,1)S(1)}, bf16[136,1536]{1,0:T(8,128)(2,1)S(1)}, u32[]{:S(2)}, u32[]{:S(2)}) collective-permute-start(bf16[136,1536]{1,0:T(8,128)(2,1)S(1)} %pad_maximum_fusion.2.refs_0_), channel_id=1, source_target_pairs={{0,14},{2,12},{4,2},{6,0},{8,6},{10,4},{12,10},{14,8},{1,15},{3,13... | collective-permute-start | bytes 1253384 | tf_op jit(solution)/shard_map/ppermute | solution.py:287
  32.9 22.5 %collective-permute-start.5 = (bf16[136,1536]{1,0:T(8,128)(2,1)S(1)}, bf16[136,1536]{1,0:T(8,128)(2,1)S(1)}, u32[]{:S(2)}, u32[]{:S(2)}) collective-permute-start(bf16[136,1536]{1,0:T(8,128)(2,1)S(1)} %pad_maximum_fusion.2.refs_0_), channel_id=1, source_target_pairs={{0,12},{2,14},{4,0},{6,2},{8,4},{10,6},{12,8},{14,10},{1,13},{3,15... | collective-permute-start | bytes 1253384 | tf_op jit(solution)/shard_map/ppermute | solution.py:287
  33.5 22.0 %collective-permute-start.4 = (bf16[136,1536]{1,0:T(8,128)(2,1)S(1)}, bf16[136,1536]{1,0:T(8,128)(2,1)}, u32[]{:S(2)}, u32[]{:S(2)}) collective-permute-start(bf16[136,1536]{1,0:T(8,128)(2,1)S(1)} %pad_maximum_fusion.2.refs_0_), channel_id=1, source_target_pairs={{0,10},{2,8},{4,14},{6,12},{8,2},{10,0},{12,6},{14,4},{1,11},{3,9}... | collective-permute-start | bytes 1253384 | tf_op jit(solution)/shard_map/ppermute | solution.py:287
  33.8 26.8 %collective-permute-start.3 = (bf16[136,1536]{1,0:T(8,128)(2,1)S(1)}, bf16[136,1536]{1,0:T(8,128)(2,1)}, u32[]{:S(2)}, u32[]{:S(2)}) collective-permute-start(bf16[136,1536]{1,0:T(8,128)(2,1)S(1)} %pad_maximum_fusion.2.refs_0_), channel_id=1, source_target_pairs={{0,8},{2,10},{4,12},{6,14},{8,0},{10,2},{12,4},{14,6},{1,9},{3,11}... | collective-permute-start | bytes 1253384 | tf_op jit(solution)/shard_map/ppermute | solution.py:287
  36.5 75.4 %copy-start.6 = (bf16[136,1536]{1,0:T(8,128)(2,1)}, bf16[136,1536]{1,0:T(8,128)(2,1)S(1)}, u32[]{:S(2)}) copy-start(bf16[136,1536]{1,0:T(8,128)(2,1)S(1)} %collective-permute-done.7.refs_8_) | copy-start | bytes 1253380
  36.5 40.3 %collective-permute-start.2 = (bf16[136,1536]{1,0:T(8,128)(2,1)S(1)}, bf16[136,1536]{1,0:T(8,128)(2,1)}, u32[]{:S(2)}, u32[]{:S(2)}) collective-permute-start(bf16[136,1536]{1,0:T(8,128)(2,1)S(1)} %pad_maximum_fusion.2.refs_0_), channel_id=1, source_target_pairs={{0,6},{2,4},{4,10},{6,8},{8,14},{10,12},{12,2},{14,0},{1,7},{3,5},... | collective-permute-start | bytes 1253384 | tf_op jit(solution)/shard_map/ppermute | solution.py:287
  43.6 68.3 %copy-start.7 = (bf16[136,1536]{1,0:T(8,128)(2,1)}, bf16[136,1536]{1,0:T(8,128)(2,1)S(1)}, u32[]{:S(2)}) copy-start(bf16[136,1536]{1,0:T(8,128)(2,1)S(1)} %collective-permute-done.6.refs_7_) | copy-start | bytes 1253380
  43.6 42.2 %collective-permute-start.1 = (bf16[136,1536]{1,0:T(8,128)(2,1)S(1)}, bf16[136,1536]{1,0:T(8,128)(2,1)}, u32[]{:S(2)}, u32[]{:S(2)}) collective-permute-start(bf16[136,1536]{1,0:T(8,128)(2,1)S(1)} %pad_maximum_fusion.2.refs_0_), channel_id=1, source_target_pairs={{0,4},{2,6},{4,8},{6,10},{8,12},{10,14},{12,0},{14,2},{1,5},{3,7},... | collective-permute-start | bytes 1253384 | tf_op jit(solution)/shard_map/ppermute | solution.py:287
  55.5 33.2 %copy-start.8 = (bf16[136,1536]{1,0:T(8,128)(2,1)}, bf16[136,1536]{1,0:T(8,128)(2,1)S(1)}, u32[]{:S(2)}) copy-start(bf16[136,1536]{1,0:T(8,128)(2,1)S(1)} %collective-permute-done.5.refs_6_) | copy-start | bytes 1253380
  55.5 31.9 %collective-permute-start = (bf16[136,1536]{1,0:T(8,128)(2,1)S(1)}, bf16[136,1536]{1,0:T(8,128)(2,1)}, u32[]{:S(2)}, u32[]{:S(2)}) collective-permute-start(bf16[136,1536]{1,0:T(8,128)(2,1)S(1)} %pad_maximum_fusion.2.refs_0_), channel_id=1, source_target_pairs={{0,2},{2,0},{4,6},{6,4},{8,10},{10,8},{12,14},{14,12},{1,3},{3,1},... | collective-permute-start | bytes 1253384 | tf_op jit(solution)/shard_map/ppermute | solution.py:287
  55.5 33.2 %collective-permute-start.14 = (bf16[136,1536]{1,0:T(8,128)(2,1)S(1)}, bf16[136,1536]{1,0:T(8,128)(2,1)S(1)}, u32[]{:S(2)}, u32[]{:S(2)}) collective-permute-start(bf16[136,1536]{1,0:T(8,128)(2,1)S(1)} %collective-permute-done.6.refs_7_), channel_id=1, source_target_pairs={{0,1},{1,0},{2,3},{3,2},{4,5},{5,4},{6,7},{7,6},{8,9},{9,8},{10,11... | collective-permute-start | bytes 1253384 | tf_op jit(solution)/shard_map/ppermute | solution.py:291
  60.5 28.3 %collective-permute-start.13 = (bf16[136,1536]{1,0:T(8,128)(2,1)S(1)}, bf16[136,1536]{1,0:T(8,128)(2,1)S(1)}, u32[]{:S(2)}, u32[]{:S(2)}) collective-permute-start(bf16[136,1536]{1,0:T(8,128)(2,1)S(1)} %collective-permute-done.5.refs_6_), channel_id=1, source_target_pairs={{0,1},{1,0},{2,3},{3,2},{4,5},{5,4},{6,7},{7,6},{8,9},{9,8},{10,11... | collective-permute-start | bytes 1253384 | tf_op jit(solution)/shard_map/ppermute | solution.py:291
  76.8 35.0 %collective-permute-start.12 = (bf16[136,1536]{1,0:T(8,128)(2,1)}, bf16[136,1536]{1,0:T(8,128)(2,1)}, u32[]{:S(2)}, u32[]{:S(2)}) collective-permute-start(bf16[136,1536]{1,0:T(8,128)(2,1)} %collective-permute-done.4.refs_5_), channel_id=1, source_target_pairs={{0,1},{1,0},{2,3},{3,2},{4,5},{5,4},{6,7},{7,6},{8,9},{9,8},{10,11... | collective-permute-start | bytes 1253384 | tf_op jit(solution)/shard_map/ppermute | solution.py:291
  85.9 26.0 %collective-permute-start.11 = (bf16[136,1536]{1,0:T(8,128)(2,1)}, bf16[136,1536]{1,0:T(8,128)(2,1)}, u32[]{:S(2)}, u32[]{:S(2)}) collective-permute-start(bf16[136,1536]{1,0:T(8,128)(2,1)} %collective-permute-done.3.refs_4_), channel_id=1, source_target_pairs={{0,1},{1,0},{2,3},{3,2},{4,5},{5,4},{6,7},{7,6},{8,9},{9,8},{10,11... | collective-permute-start | bytes 1253384 | tf_op jit(solution)/shard_map/ppermute | solution.py:291
  87.4 24.5 %collective-permute-start.10 = (bf16[136,1536]{1,0:T(8,128)(2,1)}, bf16[136,1536]{1,0:T(8,128)(2,1)}, u32[]{:S(2)}, u32[]{:S(2)}) collective-permute-start(bf16[136,1536]{1,0:T(8,128)(2,1)} %collective-permute-done.2.refs_3_), channel_id=1, source_target_pairs={{0,1},{1,0},{2,3},{3,2},{4,5},{5,4},{6,7},{7,6},{8,9},{9,8},{10,11... | collective-permute-start | bytes 1253384 | tf_op jit(solution)/shard_map/ppermute | solution.py:291
  88.7 0.8 copy-start.9
  88.7 23.2 %collective-permute-start.9 = (bf16[136,1536]{1,0:T(8,128)(2,1)}, bf16[136,1536]{1,0:T(8,128)(2,1)}, u32[]{:S(2)}, u32[]{:S(2)}) collective-permute-start(bf16[136,1536]{1,0:T(8,128)(2,1)} %collective-permute-done.1.refs_2_), channel_id=1, source_target_pairs={{0,1},{1,0},{2,3},{3,2},{4,5},{5,4},{6,7},{7,6},{8,9},{9,8},{10,11... | collective-permute-start | bytes 1253384 | tf_op jit(solution)/shard_map/ppermute | solution.py:291
  89.4 0.8 copy-start.10
  89.4 22.4 %collective-permute-start.8 = (bf16[136,1536]{1,0:T(8,128)(2,1)}, bf16[136,1536]{1,0:T(8,128)(2,1)}, u32[]{:S(2)}, u32[]{:S(2)}) collective-permute-start(bf16[136,1536]{1,0:T(8,128)(2,1)} %collective-permute-done.refs_1_), channel_id=1, source_target_pairs={{0,1},{1,0},{2,3},{3,2},{4,5},{5,4},{6,7},{7,6},{8,9},{9,8},{10,11... | collective-permute-start | bytes 1253384 | tf_op jit(solution)/shard_map/ppermute | solution.py:291
  95.0 1.3 copy-start.1
  143.8 16.2 %copy-start.2 = (bf16[3,768,384]{2,1,0:T(8,128)(2,1)S(1)}, bf16[3,768,384]{2,1,0:T(8,128)(2,1)}, u32[]{:S(2)}) copy-start(bf16[3,768,384]{2,1,0:T(8,128)(2,1)} %get-tuple-element.37) | copy-start | bytes 5308420
  160.0 8.3 %copy-start.3 = (bf16[3,768,384]{2,1,0:T(8,128)(2,1)S(1)}, bf16[3,768,384]{2,1,0:T(8,128)(2,1)}, u32[]{:S(2)}) copy-start(bf16[3,768,384]{2,1,0:T(8,128)(2,1)} %get-tuple-element.35) | copy-start | bytes 5308420
  160.0 8.3 %copy-start.4 = (bf16[3,768,384]{2,1,0:T(8,128)(2,1)S(1)}, bf16[3,768,384]{2,1,0:T(8,128)(2,1)}, u32[]{:S(2)}) copy-start(bf16[3,768,384]{2,1,0:T(8,128)(2,1)} %get-tuple-element.34) | copy-start | bytes 5308420
  162.1 6.3 %collective-permute-start.15 = (bf16[6,768,384]{2,1,0:T(8,128)(2,1)S(1)}, bf16[6,768,384]{2,1,0:T(8,128)(2,1)S(1)}, u32[]{:S(2)}, u32[]{:S(2)}) collective-permute-start(bf16[6,768,384]{2,1,0:T(8,128)(2,1)S(1)} %pad_maximum_fusion.1), channel_id=1, source_target_pairs={{0,1},{1,0},{2,3},{3,2},{4,5},{5,4},{6,7},{7,6},{8,9},{9,8},{10,11... | collective-permute-start | bytes 10616840 | tf_op jit(solution)/shard_map/ppermute | solution.py:291
  271.1 2.8 copy-start
  271.1 8.8 %collective-permute-start.16 = (bf16[6,768,384]{2,1,0:T(8,128)(2,1)S(1)}, bf16[6,768,384]{2,1,0:T(8,128)(2,1)}, u32[]{:S(2)}, u32[]{:S(2)}) collective-permute-start(bf16[6,768,384]{2,1,0:T(8,128)(2,1)S(1)} %bitcast.15), channel_id=1, source_target_pairs={{0,1},{1,0},{2,3},{3,2},{4,5},{5,4},{6,7},{7,6},{8,9},{9,8},{10,11... | collective-permute-start | bytes 10616840 | tf_op jit(solution)/shard_map/ppermute | solution.py:291

commit v2 on v1

--- a/solution.py
+++ b/solution.py
@@ -1,5 +1,3 @@
-import math
-
 import jax
 import jax.numpy as jnp
 from jax import lax
@@ -62,7 +60,7 @@
         x_o[rows, :] = buf[b, :, :D]
         bins = buf[b, :, D:D + A].astype(f32).astype(jnp.int32)
         bond = buf[b, :, D + A:].astype(f32).astype(jnp.int32)
-        own = jnp.broadcast_to(mol[pl.ds(src[b] * 8 + slot[b], 1), :].astype(f32), (A, A))
+        own = jnp.broadcast_to(mol[src[b], pl.ds(slot[b], 1), :].astype(f32), (A, A))
         idx[b] = jnp.where(own == own.T, bins + 32 * bond, 64)
     x = x_o[...]
     q_o[...] = mm(x, w_q[...]).astype(bf16) * 0.125
@@ -193,6 +191,7 @@
         out_specs=[V] * 9,
         scratch_shapes=[pltpu.VMEM((NB, A, D + 2 * A), bf16), pltpu.VMEM((NB, A, A), jnp.int32),
                         pltpu.SemaphoreType.DMA((NB,))],
+        cost_estimate=pl.CostEstimate(flops=16_000_000_000, transcendentals=0, bytes_accessed=8_000_000),
         name="self_forward",
     )(src, slot, got, mol, table, *ws, cot)
 
@@ -205,6 +204,7 @@
         out_specs=[V] * 4,
         scratch_shapes=[pltpu.VMEM((16, A + 8, 2 * D), bf16), pltpu.VMEM((R, D), bf16), pltpu.VMEM((R, D), bf16),
                         pltpu.SemaphoreType.DMA((16,))],
+        cost_estimate=pl.CostEstimate(flops=28_000_000_000, transcendentals=0, bytes_accessed=8_000_000),
         name="cross_both",
     )(chosen, me, *near, *far, cq, dc, mid, at, cot, w_co, w_cq, w_o)
 
@@ -216,32 +216,54 @@
         in_specs=[S] + [V] * 6,
         out_specs=[V] * 2,
         scratch_shapes=[pltpu.VMEM((R, 3 * D), bf16)],
+        cost_estimate=pl.CostEstimate(flops=16_000_000_000, transcendentals=0, bytes_accessed=8_000_000),
         name="self_backward",
     )(me, x, q, k, v, probs, da)
 
 
-def pack_kernel(counts, me, atoms, bins, bonds, out):
+def pack_kernel(atoms, bins, bonds, out):
     out[0, :, :D] = atoms[0]
     out[0, :, D:D + A] = bins[0].astype(f32).astype(bf16)
     out[0, :, D + A:] = bonds[0].astype(f32).astype(bf16)
 
 
-def pack_call(counts, me, atoms, bins, bonds):
-    def slot(t, counts, me):
-        offset = sum(jnp.where(d < me[3], counts[d], 0) for d in range(8))
-        return (t + 64 - offset) % 8, 0, 0
+def pack_call(atoms, bins, bonds):
+    def slot(t):
+        return t, 0, 0
 
     return pl.pallas_call(
         pack_kernel,
         out_shape=sds((8, A, D + 2 * A)),
-        grid_spec=pltpu.PrefetchScalarGridSpec(
-            num_scalar_prefetch=2,
-            grid=(8,),
-            in_specs=[pl.BlockSpec((1, A, D), slot), pl.BlockSpec((1, A, A), slot), pl.BlockSpec((1, A, A), slot)],
-            out_specs=pl.BlockSpec((1, A, D + 2 * A), lambda t, counts, me: (t, 0, 0)),
-        ),
+        grid=(8,),
+        in_specs=[pl.BlockSpec((1, A, D), slot), pl.BlockSpec((1, A, A), slot), pl.BlockSpec((1, A, A), slot)],
+        out_specs=pl.BlockSpec((1, A, D + 2 * A), slot),
         name="pack_slots",
-    )(counts, me, atoms, bins, bonds)
+    )(atoms, bins, bonds)
+
+
+def roll_kernel(counts, me, packed, out, sems):
+    offset = 0
+    for d in range(8):
+        offset = offset + jnp.where(d < me[3], counts[d, 8, 0], 0)
+    copies = [
+        pltpu.make_async_copy(packed.at[(t + 64 - offset) % 8], out.at[t], sems.at[t])
+        for t in range(8)
+    ]
+    for copy in copies:
+        copy.start()
+    for copy in copies:
+        copy.wait()
+
+
+def roll_call(counts, me, packed):
+    return pl.pallas_call(
+        roll_kernel,
+        out_shape=sds((8, A, D + 2 * A)),
+        in_specs=[S, S, ANY],
+        out_specs=ANY,
+        scratch_shapes=[pltpu.SemaphoreType.DMA((8,))],
+        name="roll_slots",
+    )(counts, me, packed)
 
 
 def index_kernel(counts, me, scaffold, ids, src_o, slot_o, chosen_o):
@@ -250,7 +272,7 @@
         rank = b * 8 + dp
         source, begin, end = 0, 0, 0
         for d in range(8):
-            end = end + counts[d]
+            end = end + counts[d, 8, 0]
             passed = (end <= rank).astype(jnp.int32)
             source = source + passed
             begin = jnp.where(passed == 1, end, begin)
@@ -272,6 +294,33 @@
     )(counts, me, scaffold, ids)
 
 
+def join_kernel(me, mine, theirs, out):
+    @pl.when(me[2] == 0)
+    def _():
+        out[0, :, :HALF] = mine[0]
+        out[0, :, HALF:] = theirs[0]
+
+    @pl.when(me[2] == 1)
+    def _():
+        out[0, :, :HALF] = theirs[0]
+        out[0, :, HALF:] = mine[0]
+
+
+def join_call(me, mine, theirs):
+    half = pl.BlockSpec((1, D, HALF), lambda i, me: (i, 0, 0))
+    return pl.pallas_call(
+        join_kernel,
+        out_shape=sds((6, D, D)),
+        grid_spec=pltpu.PrefetchScalarGridSpec(
+            num_scalar_prefetch=1,
+            grid=(6,),
+            in_specs=[half, half],
+            out_specs=pl.BlockSpec((1, D, D), lambda i, me: (i, 0, 0)),
+        ),
+        name="join_halves",
+    )(me, mine, theirs)
+
+
 CHIPS = ("z", "yl", "x", "yh")
 
 
@@ -298,7 +347,7 @@
     return exchange(jnp.broadcast_to(total[None], pieces.shape), CHIPS).reshape(-1, D, HALF)
 
 
-def on_device(
+def layer(
     atoms, distance_bins, bonds, molecule, block_counts, block_scaffold, pocket_ids, pocket_keys, pocket_values,
     pocket_bias, bin_table, bond_weight, w_query, w_key, w_value, w_out, w_cross_query, w_cross_out, cotangent,
 ):
@@ -306,9 +355,9 @@
     me = jnp.stack([x, yh, c, z * 2 + yl, x * 4 + yh * 2 + c]).astype(jnp.int32)
     note = jnp.concatenate([molecule, jnp.broadcast_to(block_counts, (8, A))], axis=0)
     notes = exchange(jnp.broadcast_to(note[None], (8, 16, A)), ("z", "yl"))
-    counts = notes[:, 8, 0]
-    mol = notes[:, :8].reshape(64, A)
-    got = exchange(pack_call(counts, me, atoms, distance_bins, bonds), ("z", "yl"))
+    packed = pack_call(atoms, distance_bins, bonds)
+    rolled = roll_call(notes, me, packed)
+    got = exchange(rolled, ("z", "yl"))
     pocket = jnp.concatenate(
         [
             jnp.concatenate([pocket_keys, pocket_values], axis=1),
@@ -316,9 +365,15 @@
         ],
         axis=0,
     )
-    near = [pocket if i == 0 else shifted(pocket, i // 2, i % 2) for i in range(8)]
-    far = [swap_core(n) for n in near]
-    src, slot, chosen = index_call(counts, me, block_scaffold, pocket_ids.T)
+    mirror = shifted(pocket, 0, 1)
+    near = [pocket, mirror]
+    for i in range(1, 4):
+        near.append(shifted(pocket, i, 0))
+        near.append(shifted(mirror, i, 0))
+    far = []
+    for i in range(8):
+        far.append(swap_core(near[i]))
+    src, slot, chosen = index_call(notes, me, block_scaffold, pocket_ids.T)
     table = jnp.concatenate(
         [
             bin_table,
@@ -330,16 +385,14 @@
     table = lax.reduce_precision(table, 8, 7)
     cot = cotangent.reshape(R, D)
     ws = (w_query, w_key, w_value, w_out, w_cross_query, w_cross_out)
-    xs, q, k, v, probs, at, mid, cq, dc = self_call(src, slot, got, mol, table, ws, cot)
+    xs, q, k, v, probs, at, mid, cq, dc = self_call(src, slot, got, notes, table, ws, cot)
     updated, da, keep_a, send_a = cross_call(
         chosen, me, near, far, cq, dc, mid, at, cot, w_cross_out, w_cross_query, w_out
     )
     keep_b, send_b = back_call(me, xs, q, k, v, probs, da)
     mine = reduce_grads(jnp.concatenate([keep_b, keep_a]), jnp.concatenate([send_b, send_a]))
     theirs = swap_core(mine)
-    low = jnp.where(c == 0, mine, theirs)
-    high = jnp.where(c == 0, theirs, mine)
-    return updated.reshape(cotangent.shape), jnp.concatenate([low, high], axis=2)
+    return updated.reshape(cotangent.shape), join_call(me, mine, theirs)
 
 
 def solution(mesh):
@@ -347,7 +400,7 @@
     every = ("z", "yl", "x", "yh", "c")
     pocket = ("x", "yh", "c")
     return jax.shard_map(
-        on_device,
+        layer,
         mesh=fine,
         in_specs=(
             P(every, None, None),

time: 292 us -> 339 us (1.16)
  Pallas kernels: 73.8 us -> 148 us
  other arithmetic: 15.4 us -> 4.27 us
  waiting for transfers between devices: 51.6 us -> 41.2 us
    pallas_call x1 -> x3, Pallas kernels: 6.65 us -> 80.2 us  [the longest x1 66.5 us: roll_call(): pl.pallas_call(roll_kernel, out_shape=sds((8, A, D + 2 * A)), in_specs=[S...]
    ppermute x7, waiting for transfers between devices: 34.9 us -> 29 us  [shifted(): return lax.ppermute(matrix, ('x', 'yh'), pairs)]
    concatenate x3 -> x2, other arithmetic: 7.62 us -> 2.06 us  [the longest x1 2.03 us: layer(): jnp.concatenate([send_b, send_a])]
    select_n x1 -> x0, other arithmetic: 5.54 us -> none  [on_device(): low = jnp.where(c == 0, mine, theirs)]
    all_to_all x2, waiting for transfers between devices: 4.53 us -> 0.01 us  [exchange(): return lax.all_to_all(matrix, axes, split_axis=0, concat_axis=0, tiled=True)]
  transfers between devices with their start and end apart: 19 -> 19, of which waited for: 8 -> 4; matrix products, arithmetic and copies ran while one was open for 1% -> 0% of each run, Pallas kernels for 7% -> 8%
where the time goes in v2:
time: 339 us; the launch traced here: 338 us
  Pallas kernels  148 us (44%)
  blocking collectives  98.9 us (29%)
  waiting for transfers between devices  41.2 us (12%)
  starting transfers between devices  39.4 us (12%)
  local copies, waits for them, and re-layouts  4.35 us (1%)
  other arithmetic  4.27 us (1%)
    all_to_all x2, blocking collectives, exchange(): return lax.all_to_all(matrix, axes, split_axis=0, concat_axis=0, tiled=True)  98.9 us
    pallas_call x1, Pallas kernels, roll_call(): pl.pallas_call(roll_kernel, out_shape=sds((8, A, D + 2 * A)), in_specs=[S...  66.5 us
    pallas_call x1, Pallas kernels, cross_call(): pl.pallas_call(cross_kernel, out_shape=[sds((R, D)), sds((R, D)), sds((3,...  31.8 us
    ppermute x7, waiting for transfers between devices, shifted(): return lax.ppermute(matrix, ('x', 'yh'), pairs)  29 us
    ppermute x10, starting transfers between devices, swap_core(): return lax.ppermute(matrix, 'c', [(0, 1), (1, 0)])  17.5 us
    pallas_call x1, Pallas kernels, back_call(): pl.pallas_call(back_kernel, out_shape=[sds((3, D, HALF)), sds((3, D, HALF...  16.1 us
    pallas_call x1, Pallas kernels, self_call(): pl.pallas_call(self_kernel, out_shape=[sds((R, D)) for _ in range(4)] + [...  15.6 us
    ppermute x10, waiting for transfers between devices, swap_core(): return lax.ppermute(matrix, 'c', [(0, 1), (1, 0)])  12.2 us
  transfers between devices with their start and end apart: 19, of which 4 were waited for; matrix products, arithmetic and copies ran while one was open for 0% of the time, Pallas kernels for 8%

profile of v2, /device:TPU:1, one launch (start us, length us, event | category | flops | bytes accessed | tf_op | source)
XLA Modules:
  0.0 337.9 jit_solution(13376125465117656510)
XLA Ops:
  1.3 0.7 concatenate.18
  2.0 0.6 broadcast_in_dim.13
  2.6 6.9 %all-to-all-start = ((s32[8,16,128]{2,1,0:T(8,128)}), s32[8,16,128]{2,1,0:T(8,128)S(1)}, u32[]{:S(2)}, u32[]{:S(2)}) async-start(s32[8,16,128]{2,1,0:T(8,128)} %broadcast_in_dim.13), calls=%async_computation | async-start | bytes 131072 | tf_op jit(solution)/shard_map/all_to_all | solution.py:328
  9.5 5.8 %pack_slots.1.packed = bf16[8,128,1024]{2,1,0:T(8,128)(2,1)} custom-call(bf16[8,128,768]{2,1,0:T(8,128)(2,1)} %atoms.1, s32[8,128,128]{2,1,0:T(8,128)} %bins.1, s32[8,128,128]{2,1,0:T(8,128)} %bonds.1), custom_call_target="tpu_custom_call" | custom-call | tf_op jit(solution)/shard_map/pack_slots/pallas_call | solution.py:234
  15.3 0.7 stack.23.me
  15.9 0.0 all-to-all-done.counts.mol
  15.9 0.0 copy-start.5
  15.9 0.6 copy-done.5
  16.6 66.5 %roll_slots.1 = bf16[8,128,1024]{2,1,0:T(8,128)(2,1)} custom-call(s32[8,16,128]{2,1,0:T(8,128)} %copy-done.5, s32[5]{0:T(128)} %stack.23.me, bf16[8,128,1024]{2,1,0:T(8,128)(2,1)} %pack_slots.1.packed), custom_call_target="tpu_custom_call" | custom-call | tf_op jit(solution)/shard_map/roll_slots/pallas_call | solution.py:259
  83.0 0.0 copy-start.9
  83.0 0.0 copy-start.11
  83.1 5.1 %all-to-all-start.1 = ((bf16[8,128,1024]{2,1,0:T(8,128)(2,1)}), bf16[8,128,1024]{2,1,0:T(8,128)(2,1)S(1)}, u32[]{:S(2)}, u32[]{:S(2)}) async-start(bf16[8,128,1024]{2,1,0:T(8,128)(2,1)} %roll_slots.1), calls=%async_computation.1 | async-start | bytes 4194304 | tf_op jit(solution)/shard_map/all_to_all | solution.py:328
  88.3 2.7 collective-permute-start
  91.0 1.8 collective-permute-start.7
  92.8 2.5 collective-permute-start.5
  95.3 0.5 collective-permute-start.3
  95.8 0.6 collective-permute-start.1
  96.4 0.1 pad.7.clone
  96.5 25.7 %collective-permute-done.refs_1_ = bf16[136,1536]{1,0:T(8,128)(2,1)S(1)} collective-permute-done((bf16[136,1536]{1,0:T(8,128)(2,1)S(1)}, bf16[136,1536]{1,0:T(8,128)(2,1)S(1)}, u32[]{:S(2)}, u32[]{:S(2)}) %collective-permute-start) | collective-permute-done | bytes 417824 | tf_op jit(solution)/shard_map/ppermute | solution.py:336
  122.2 2.5 collective-permute-start.6
  124.7 0.5 collective-permute-start.4
  125.2 0.6 collective-permute-start.2
  125.8 2.9 collective-permute-start.13
  128.7 0.1 collective-permute-start.11
  128.8 0.1 broadcast_add_fusion
  128.9 0.7 maximum_reduce-precision_fusion.table
  129.6 4.6 %find_blocks.1 = (s32[4]{0:T(128)}, s32[4]{0:T(128)}, s32[16]{0:T(128)}) custom-call(s32[8,16,128]{2,1,0:T(8,128)} %copy-done.5, s32[5]{0:T(128)} %stack.23.me, s32[1024]{0:T(1024)} %scaffold.1, s32[4,8192]{1,0:T(4,128)} %bitcast.16), custom_call_target="tpu_custom_call" | custom-call | tf_op jit(solution)/shard_map/find_blocks/pallas_call | solution.py:288
  134.2 0.5 collective-permute-start.8
  134.7 0.1 collective-permute-start.9
  134.8 8.7 %collective-permute-start.14 = (bf16[136,1536]{1,0:T(8,128)(2,1)}, bf16[136,1536]{1,0:T(8,128)(2,1)}, u32[]{:S(2)}, u32[]{:S(2)}) collective-permute-start(bf16[136,1536]{1,0:T(8,128)(2,1)} %collective-permute-done.6.refs_7_), channel_id=1, source_target_pairs={{0,1},{1,0},{2,3},{3,2},{4,5},{5,4},{6,7},{7,6},{8,9},{9,8},{10,11... | collective-permute-start | bytes 1253384 | tf_op jit(solution)/shard_map/ppermute | solution.py:340
  143.5 0.0 collective-permute-start.12
  143.5 3.3 collective-permute-done.2.refs_3_
  146.8 0.5 collective-permute-start.10
  147.3 1.3 copy-done.1
  148.6 15.6 %self_forward.1 = (bf16[512,768]{1,0:T(8,128)(2,1)}, bf16[512,768]{1,0:T(8,128)(2,1)}, bf16[512,768]{1,0:T(8,128)(2,1)}, bf16[512,768]{1,0:T(8,128)(2,1)}, f32[4...) custom-call(s32[4]{0:T(128)} %get-tuple-element.21.src, ...), custom_call_target="tpu_custom_call" | custom-call | flops 16000000000 | bytes 8000000 | tf_op jit(solution)/shard_map/self_forward/pallas_call | solution.py:187
  164.2 31.8 %cross_both.1 = (bf16[512,768]{1,0:T(8,128)(2,1)}, bf16[512,768]{1,0:T(8,128)(2,1)}, bf16[3,768,384]{2,1,0:T(8,128)(2,1)}, bf16[3,768,384]{2,1,0:T(8,128)(2,1)}) custom-call(s32[16]{0:T(128)} %get-tuple-element.20.chosen, s32[5]{0:T(128)} %stack.23.me, bf16[136,1536]{1,0:T(8,128)(2,1)} %copy-done.6, bf16[136,1536]{1,0:T(8,128)(2,1)} %copy-done.12, ...), custom_call_target="tpu_custom_call" | custom-call | flops 28000000000 | bytes 8000000 | tf_op jit(solution)/shard_map/cross_both/pallas_call | solution.py:200
  196.1 16.1 %self_backward.1 = (bf16[3,768,384]{2,1,0:T(8,128)(2,1)}, bf16[3,768,384]{2,1,0:T(8,128)(2,1)}) custom-call(s32[5]{0:T(128)} %stack.23.me, bf16[512,768]{1,0:T(8,128)(2,1)} %get-tuple-element.28.x, bf16[512,768]{1,0:T(8,128)(2,1)} %get-tuple-element.29.q, bf16[512,768]{1,0:T(8,128)(2,1)} %get-tuple-element.30.k, bf16[512,768]{1,0:T(8,128)(2,1)} %get-tuple-element.31.v, ...), custom_call_target="tpu_custom_call" | custom-call | flops 16000000000 | bytes 8000000 | tf_op jit(solution)/shard_map/self_backward/pallas_call | solution.py:213
  212.1 2.0 pad_maximum_fusion
  214.2 0.1 collective-permute-start.15
  214.3 6.2 %collective-permute-done.15 = bf16[6,768,384]{2,1,0:T(8,128)(2,1)S(1)} collective-permute-done((bf16[6,768,384]{2,1,0:T(8,128)(2,1)S(1)}, bf16[6,768,384]{2,1,0:T(8,128)(2,1)S(1)}, u32[]{:S(2)}, u32[]{:S(2)}) %collective-permute-start.15) | collective-permute-done | bytes 3538976 | tf_op jit(solution)/shard_map/ppermute | solution.py:340
  220.5 1.0 add_convert_fusion
  221.4 50.7 %all_to_all.20 = bf16[64,72,384]{2,1,0:T(8,128)(2,1)S(1)} all-to-all(bf16[64,72,384]{2,1,0:T(8,128)(2,1)S(1)} %bitcast.15), channel_id=1, replica_groups=mesh['z'=4,'yl'=2,'x'=4,'yh'=2,'c'=2] {'z','yl','x','yh'}, dimensions={0} | all-to-all | bytes 7077888 | tf_op jit(solution)/shard_map/all_to_all | solution.py:328
  272.2 0.5 convert_reduce_fusion
  272.7 0.3 broadcast_in_dim.33
  273.0 48.2 %all_to_all.21 = bf16[64,72,384]{2,1,0:T(8,128)(2,1)S(1)} all-to-all(bf16[64,72,384]{2,1,0:T(8,128)(2,1)S(1)} %broadcast_in_dim.33), channel_id=1, replica_groups=mesh['z'=4,'yl'=2,'x'=4,'yh'=2,'c'=2] {'z','yl','x','yh'}, dimensions={0} | all-to-all | bytes 7077888 | tf_op jit(solution)/shard_map/all_to_all | solution.py:328
  321.2 2.8 collective-permute-start.16
  324.0 6.0 %collective-permute-done.16.theirs = bf16[6,768,384]{2,1,0:T(8,128)(2,1)} collective-permute-done((bf16[6,768,384]{2,1,0:T(8,128)(2,1)S(1)}, bf16[6,768,384]{2,1,0:T(8,128)(2,1)}, u32[]{:S(2)}, u32[]{:S(2)}) %collective-permute-start.16) | collective-permute-done | bytes 3538976 | tf_op jit(solution)/shard_map/ppermute | solution.py:340
  330.0 7.9 %join_halves.1 = bf16[6,768,768]{2,1,0:T(8,128)(2,1)} custom-call(s32[5]{0:T(128)} %stack.23.me, bf16[6,768,384]{2,1,0:T(8,128)(2,1)} %bitcast.14, bf16[6,768,384]{2,1,0:T(8,128)(2,1)} %collective-permute-done.16.theirs), custom_call_target="tpu_custom_call" | custom-call | tf_op jit(solution)/shard_map/join_halves/pallas_call | solution.py:311
  (43 shorter events, 0.1 us)
Async XLA Ops:
  2.6 13.3 %all-to-all-start = ((s32[8,16,128]{2,1,0:T(8,128)}), s32[8,16,128]{2,1,0:T(8,128)S(1)}, u32[]{:S(2)}, u32[]{:S(2)}) async-start(s32[8,16,128]{2,1,0:T(8,128)} %broadcast_in_dim.13), calls=%async_computation | async-start | bytes 131072 | tf_op jit(solution)/shard_map/all_to_all | solution.py:328
  15.9 72.3 %copy-start.10 = (bf16[12,128]{1,0:T(8,128)(2,1)S(1)}, bf16[12,128]{1,0:T(8,128)(2,1)}, u32[]{:S(2)}) copy-start(bf16[12,128]{1,0:T(8,128)(2,1)} %param.28) | copy-start | bytes 9220
  15.9 72.3 %copy-start.7 = (bf16[128,768]{1,0:T(8,128)(2,1)S(1)}, bf16[128,768]{1,0:T(8,128)(2,1)}, u32[]{:S(2)}) copy-start(bf16[128,768]{1,0:T(8,128)(2,1)} %param.27) | copy-start | bytes 589828
  15.9 72.3 %copy-start.8 = (bf16[128,768]{1,0:T(8,128)(2,1)S(1)}, bf16[128,768]{1,0:T(8,128)(2,1)}, u32[]{:S(2)}) copy-start(bf16[128,768]{1,0:T(8,128)(2,1)} %param.26) | copy-start | bytes 589828
  15.9 0.6 copy-start.5
  83.0 45.8 %copy-start.9 = (f32[12,32]{1,0:T(8,128)S(1)}, f32[12,32]{1,0:T(8,128)}, u32[]{:S(2)}) copy-start(f32[12,32]{1,0:T(8,128)} %param.29) | copy-start | bytes 4612
  83.0 45.8 %copy-start.11 = (f32[12]{0:T(128)S(1)}, f32[12]{0:T(128)}, u32[]{:S(2)}) copy-start(f32[12]{0:T(128)} %param.30) | copy-start | bytes 148
  83.1 64.2 %all-to-all-start.1 = ((bf16[8,128,1024]{2,1,0:T(8,128)(2,1)}), bf16[8,128,1024]{2,1,0:T(8,128)(2,1)S(1)}, u32[]{:S(2)}, u32[]{:S(2)}) async-start(bf16[8,128,1024]{2,1,0:T(8,128)(2,1)} %roll_slots.1), calls=%async_computation.1 | async-start | bytes 4194304 | tf_op jit(solution)/shard_map/all_to_all | solution.py:328
  88.3 75.9 %copy-start.6 = (bf16[136,1536]{1,0:T(8,128)(2,1)}, bf16[136,1536]{1,0:T(8,128)(2,1)S(1)}, u32[]{:S(2)}) copy-start(bf16[136,1536]{1,0:T(8,128)(2,1)S(1)} %pad_maximum_fusion.1.refs_0_) | copy-start | bytes 1253380
  88.3 33.9 %collective-permute-start = (bf16[136,1536]{1,0:T(8,128)(2,1)S(1)}, bf16[136,1536]{1,0:T(8,128)(2,1)S(1)}, u32[]{:S(2)}, u32[]{:S(2)}) collective-permute-start(bf16[136,1536]{1,0:T(8,128)(2,1)S(1)} %pad_maximum_fusion.1.refs_0_), channel_id=1, source_target_pairs={{0,2},{2,0},{4,6},{6,4},{8,10},{10,8},{12,14},{14,12},{1,3},{3,1},... | collective-permute-start | bytes 1253384 | tf_op jit(solution)/shard_map/ppermute | solution.py:336
  91.0 33.7 %collective-permute-start.7 = (bf16[136,1536]{1,0:T(8,128)(2,1)S(1)}, bf16[136,1536]{1,0:T(8,128)(2,1)S(1)}, u32[]{:S(2)}, u32[]{:S(2)}) collective-permute-start(bf16[136,1536]{1,0:T(8,128)(2,1)S(1)} %pad_maximum_fusion.1.refs_0_), channel_id=1, source_target_pairs={{0,1},{1,0},{2,3},{3,2},{4,5},{5,4},{6,7},{7,6},{8,9},{9,8},{10,11... | collective-permute-start | bytes 1253384 | tf_op jit(solution)/shard_map/ppermute | solution.py:340
  92.8 32.4 %collective-permute-start.5 = (bf16[136,1536]{1,0:T(8,128)(2,1)S(1)}, bf16[136,1536]{1,0:T(8,128)(2,1)}, u32[]{:S(2)}, u32[]{:S(2)}) collective-permute-start(bf16[136,1536]{1,0:T(8,128)(2,1)S(1)} %pad_maximum_fusion.1.refs_0_), channel_id=1, source_target_pairs={{0,12},{2,14},{4,0},{6,2},{8,4},{10,6},{12,8},{14,10},{1,13},{3,15... | collective-permute-start | bytes 1253384 | tf_op jit(solution)/shard_map/ppermute | solution.py:336
  95.3 30.5 %collective-permute-start.3 = (bf16[136,1536]{1,0:T(8,128)(2,1)S(1)}, bf16[136,1536]{1,0:T(8,128)(2,1)}, u32[]{:S(2)}, u32[]{:S(2)}) collective-permute-start(bf16[136,1536]{1,0:T(8,128)(2,1)S(1)} %pad_maximum_fusion.1.refs_0_), channel_id=1, source_target_pairs={{0,8},{2,10},{4,12},{6,14},{8,0},{10,2},{12,4},{14,6},{1,9},{3,11}... | collective-permute-start | bytes 1253384 | tf_op jit(solution)/shard_map/ppermute | solution.py:336
  95.8 32.9 %collective-permute-start.1 = (bf16[136,1536]{1,0:T(8,128)(2,1)S(1)}, bf16[136,1536]{1,0:T(8,128)(2,1)S(1)}, u32[]{:S(2)}, u32[]{:S(2)}) collective-permute-start(bf16[136,1536]{1,0:T(8,128)(2,1)S(1)} %pad_maximum_fusion.1.refs_0_), channel_id=1, source_target_pairs={{0,4},{2,6},{4,8},{6,10},{8,12},{10,14},{12,0},{14,2},{1,5},{3,7},... | collective-permute-start | bytes 1253384 | tf_op jit(solution)/shard_map/ppermute | solution.py:336
  122.2 42.0 %copy-start.12 = (bf16[136,1536]{1,0:T(8,128)(2,1)}, bf16[136,1536]{1,0:T(8,128)(2,1)S(1)}, u32[]{:S(2)}) copy-start(bf16[136,1536]{1,0:T(8,128)(2,1)S(1)} %collective-permute-done.refs_1_) | copy-start | bytes 1253380
  122.2 12.6 %collective-permute-start.6 = (bf16[136,1536]{1,0:T(8,128)(2,1)S(1)}, bf16[136,1536]{1,0:T(8,128)(2,1)}, u32[]{:S(2)}, u32[]{:S(2)}) collective-permute-start(bf16[136,1536]{1,0:T(8,128)(2,1)S(1)} %collective-permute-done.refs_1_), channel_id=1, source_target_pairs={{0,12},{2,14},{4,0},{6,2},{8,4},{10,6},{12,8},{14,10},{1,13},{3,15... | collective-permute-start | bytes 1253384 | tf_op jit(solution)/shard_map/ppermute | solution.py:336
  124.7 4.9 %copy-start.13 = (bf16[136,1536]{1,0:T(8,128)(2,1)}, bf16[136,1536]{1,0:T(8,128)(2,1)S(1)}, u32[]{:S(2)}) copy-start(bf16[136,1536]{1,0:T(8,128)(2,1)S(1)} %collective-permute-done.7.refs_8_) | copy-start | bytes 1253380
  124.7 18.8 %collective-permute-start.4 = (bf16[136,1536]{1,0:T(8,128)(2,1)S(1)}, bf16[136,1536]{1,0:T(8,128)(2,1)}, u32[]{:S(2)}, u32[]{:S(2)}) collective-permute-start(bf16[136,1536]{1,0:T(8,128)(2,1)S(1)} %collective-permute-done.refs_1_), channel_id=1, source_target_pairs={{0,8},{2,10},{4,12},{6,14},{8,0},{10,2},{12,4},{14,6},{1,9},{3,11}... | collective-permute-start | bytes 1253384 | tf_op jit(solution)/shard_map/ppermute | solution.py:336
  125.2 21.6 %collective-permute-start.2 = (bf16[136,1536]{1,0:T(8,128)(2,1)S(1)}, bf16[136,1536]{1,0:T(8,128)(2,1)}, u32[]{:S(2)}, u32[]{:S(2)}) collective-permute-start(bf16[136,1536]{1,0:T(8,128)(2,1)S(1)} %collective-permute-done.refs_1_), channel_id=1, source_target_pairs={{0,4},{2,6},{4,8},{6,10},{8,12},{10,14},{12,0},{14,2},{1,5},{3,7},... | collective-permute-start | bytes 1253384 | tf_op jit(solution)/shard_map/ppermute | solution.py:336
  125.8 8.4 %collective-permute-start.13 = (bf16[136,1536]{1,0:T(8,128)(2,1)}, bf16[136,1536]{1,0:T(8,128)(2,1)}, u32[]{:S(2)}, u32[]{:S(2)}) collective-permute-start(bf16[136,1536]{1,0:T(8,128)(2,1)} %collective-permute-done.5.refs_6_), channel_id=1, source_target_pairs={{0,1},{1,0},{2,3},{3,2},{4,5},{5,4},{6,7},{7,6},{8,9},{9,8},{10,11... | collective-permute-start | bytes 1253384 | tf_op jit(solution)/shard_map/ppermute | solution.py:340
  128.7 35.4 %copy-start.14 = (bf16[136,1536]{1,0:T(8,128)(2,1)}, bf16[136,1536]{1,0:T(8,128)(2,1)S(1)}, u32[]{:S(2)}) copy-start(bf16[136,1536]{1,0:T(8,128)(2,1)S(1)} %collective-permute-done.1.refs_2_) | copy-start | bytes 1253380
  128.7 6.0 %collective-permute-start.11 = (bf16[136,1536]{1,0:T(8,128)(2,1)}, bf16[136,1536]{1,0:T(8,128)(2,1)}, u32[]{:S(2)}, u32[]{:S(2)}) collective-permute-start(bf16[136,1536]{1,0:T(8,128)(2,1)} %collective-permute-done.3.refs_4_), channel_id=1, source_target_pairs={{0,1},{1,0},{2,3},{3,2},{4,5},{5,4},{6,7},{7,6},{8,9},{9,8},{10,11... | collective-permute-start | bytes 1253384 | tf_op jit(solution)/shard_map/ppermute | solution.py:340
  134.2 30.0 %collective-permute-start.8 = (bf16[136,1536]{1,0:T(8,128)(2,1)S(1)}, bf16[136,1536]{1,0:T(8,128)(2,1)}, u32[]{:S(2)}, u32[]{:S(2)}) collective-permute-start(bf16[136,1536]{1,0:T(8,128)(2,1)S(1)} %collective-permute-done.refs_1_), channel_id=1, source_target_pairs={{0,1},{1,0},{2,3},{3,2},{4,5},{5,4},{6,7},{7,6},{8,9},{9,8},{10,11... | collective-permute-start | bytes 1253384 | tf_op jit(solution)/shard_map/ppermute | solution.py:340
  134.7 29.5 %collective-permute-start.9 = (bf16[136,1536]{1,0:T(8,128)(2,1)S(1)}, bf16[136,1536]{1,0:T(8,128)(2,1)}, u32[]{:S(2)}, u32[]{:S(2)}) collective-permute-start(bf16[136,1536]{1,0:T(8,128)(2,1)S(1)} %collective-permute-done.1.refs_2_), channel_id=1, source_target_pairs={{0,1},{1,0},{2,3},{3,2},{4,5},{5,4},{6,7},{7,6},{8,9},{9,8},{10,11... | collective-permute-start | bytes 1253384 | tf_op jit(solution)/shard_map/ppermute | solution.py:340
  134.8 29.4 %collective-permute-start.14 = (bf16[136,1536]{1,0:T(8,128)(2,1)}, bf16[136,1536]{1,0:T(8,128)(2,1)}, u32[]{:S(2)}, u32[]{:S(2)}) collective-permute-start(bf16[136,1536]{1,0:T(8,128)(2,1)} %collective-permute-done.6.refs_7_), channel_id=1, source_target_pairs={{0,1},{1,0},{2,3},{3,2},{4,5},{5,4},{6,7},{7,6},{8,9},{9,8},{10,11... | collective-permute-start | bytes 1253384 | tf_op jit(solution)/shard_map/ppermute | solution.py:340
  143.5 20.7 %collective-permute-start.12 = (bf16[136,1536]{1,0:T(8,128)(2,1)}, bf16[136,1536]{1,0:T(8,128)(2,1)}, u32[]{:S(2)}, u32[]{:S(2)}) collective-permute-start(bf16[136,1536]{1,0:T(8,128)(2,1)} %collective-permute-done.4.refs_5_), channel_id=1, source_target_pairs={{0,1},{1,0},{2,3},{3,2},{4,5},{5,4},{6,7},{7,6},{8,9},{9,8},{10,11... | collective-permute-start | bytes 1253384 | tf_op jit(solution)/shard_map/ppermute | solution.py:340
  146.8 17.4 %collective-permute-start.10 = (bf16[136,1536]{1,0:T(8,128)(2,1)}, bf16[136,1536]{1,0:T(8,128)(2,1)}, u32[]{:S(2)}, u32[]{:S(2)}) collective-permute-start(bf16[136,1536]{1,0:T(8,128)(2,1)} %collective-permute-done.2.refs_3_), channel_id=1, source_target_pairs={{0,1},{1,0},{2,3},{3,2},{4,5},{5,4},{6,7},{7,6},{8,9},{9,8},{10,11... | collective-permute-start | bytes 1253384 | tf_op jit(solution)/shard_map/ppermute | solution.py:340
  147.3 1.3 copy-start.1
  196.1 16.1 %copy-start.2 = (bf16[3,768,384]{2,1,0:T(8,128)(2,1)S(1)}, bf16[3,768,384]{2,1,0:T(8,128)(2,1)}, u32[]{:S(2)}) copy-start(bf16[3,768,384]{2,1,0:T(8,128)(2,1)} %get-tuple-element.37) | copy-start | bytes 5308420
  212.1 8.3 %copy-start.3 = (bf16[3,768,384]{2,1,0:T(8,128)(2,1)S(1)}, bf16[3,768,384]{2,1,0:T(8,128)(2,1)}, u32[]{:S(2)}) copy-start(bf16[3,768,384]{2,1,0:T(8,128)(2,1)} %get-tuple-element.35) | copy-start | bytes 5308420
  212.1 8.3 %copy-start.4 = (bf16[3,768,384]{2,1,0:T(8,128)(2,1)S(1)}, bf16[3,768,384]{2,1,0:T(8,128)(2,1)}, u32[]{:S(2)}) copy-start(bf16[3,768,384]{2,1,0:T(8,128)(2,1)} %get-tuple-element.34) | copy-start | bytes 5308420
  214.2 6.3 %collective-permute-start.15 = (bf16[6,768,384]{2,1,0:T(8,128)(2,1)S(1)}, bf16[6,768,384]{2,1,0:T(8,128)(2,1)S(1)}, u32[]{:S(2)}, u32[]{:S(2)}) collective-permute-start(bf16[6,768,384]{2,1,0:T(8,128)(2,1)S(1)} %pad_maximum_fusion), channel_id=1, source_target_pairs={{0,1},{1,0},{2,3},{3,2},{4,5},{5,4},{6,7},{7,6},{8,9},{9,8},{10,11... | collective-permute-start | bytes 10616840 | tf_op jit(solution)/shard_map/ppermute | solution.py:340
  321.2 8.8 %copy-start = (bf16[64,72,384]{2,1,0:T(8,128)(2,1)}, bf16[64,72,384]{2,1,0:T(8,128)(2,1)S(1)}, u32[]{:S(2)}) copy-start(bf16[64,72,384]{2,1,0:T(8,128)(2,1)S(1)} %all_to_all.21) | copy-start | bytes 10616836
  321.2 8.8 %collective-permute-start.16 = (bf16[6,768,384]{2,1,0:T(8,128)(2,1)S(1)}, bf16[6,768,384]{2,1,0:T(8,128)(2,1)}, u32[]{:S(2)}, u32[]{:S(2)}) collective-permute-start(bf16[6,768,384]{2,1,0:T(8,128)(2,1)S(1)} %bitcast.13), channel_id=1, source_target_pairs={{0,1},{1,0},{2,3},{3,2},{4,5},{5,4},{6,7},{7,6},{8,9},{9,8},{10,11... | collective-permute-start | bytes 10616840 | tf_op jit(solution)/shard_map/ppermute | solution.py:340

commit v3 on v2

--- a/solution.py
+++ b/solution.py
@@ -13,6 +13,7 @@
 NB = 4
 T = 512
 HALF = D // 2
+ROWS = D // 4
 
 
 def mm(a, b):
@@ -221,49 +222,30 @@
     )(me, x, q, k, v, probs, da)
 
 
-def pack_kernel(atoms, bins, bonds, out):
-    out[0, :, :D] = atoms[0]
-    out[0, :, D:D + A] = bins[0].astype(f32).astype(bf16)
-    out[0, :, D + A:] = bonds[0].astype(f32).astype(bf16)
-
-
-def pack_call(atoms, bins, bonds):
-    def slot(t):
-        return t, 0, 0
-
-    return pl.pallas_call(
-        pack_kernel,
-        out_shape=sds((8, A, D + 2 * A)),
-        grid=(8,),
-        in_specs=[pl.BlockSpec((1, A, D), slot), pl.BlockSpec((1, A, A), slot), pl.BlockSpec((1, A, A), slot)],
-        out_specs=pl.BlockSpec((1, A, D + 2 * A), slot),
-        name="pack_slots",
-    )(atoms, bins, bonds)
-
-
-def roll_kernel(counts, me, packed, out, sems):
+def roll_kernel(notes, me, atoms, codes, out, sems):
     offset = 0
     for d in range(8):
-        offset = offset + jnp.where(d < me[3], counts[d, 8, 0], 0)
-    copies = [
-        pltpu.make_async_copy(packed.at[(t + 64 - offset) % 8], out.at[t], sems.at[t])
-        for t in range(8)
-    ]
+        offset = offset + jnp.where(d < me[3], notes[d, 8, 0], 0)
+    copies = []
+    for t in range(8):
+        slot = (t + 64 - offset) % 8
+        copies.append(pltpu.make_async_copy(atoms.at[slot], out.at[t, :, pl.ds(0, D)], sems.at[t]))
+        copies.append(pltpu.make_async_copy(codes.at[slot], out.at[t, :, pl.ds(D, 2 * A)], sems.at[8 + t]))
     for copy in copies:
         copy.start()
     for copy in copies:
         copy.wait()
 
 
-def roll_call(counts, me, packed):
+def roll_call(notes, me, atoms, codes):
     return pl.pallas_call(
         roll_kernel,
         out_shape=sds((8, A, D + 2 * A)),
-        in_specs=[S, S, ANY],
-        out_specs=ANY,
-        scratch_shapes=[pltpu.SemaphoreType.DMA((8,))],
+        in_specs=[S, S, ANY, ANY],
+        out_specs=V,
+        scratch_shapes=[pltpu.SemaphoreType.DMA((16,))],
         name="roll_slots",
-    )(counts, me, packed)
+    )(notes, me, atoms, codes)
 
 
 def index_kernel(counts, me, scaffold, ids, src_o, slot_o, chosen_o):
@@ -294,34 +276,91 @@
     )(counts, me, scaffold, ids)
 
 
-def join_kernel(me, mine, theirs, out):
-    @pl.when(me[2] == 0)
-    def _():
-        out[0, :, :HALF] = mine[0]
-        out[0, :, HALF:] = theirs[0]
-
-    @pl.when(me[2] == 1)
-    def _():
-        out[0, :, :HALF] = theirs[0]
-        out[0, :, HALF:] = mine[0]
+def fold_kernel(me, *refs):
+    keep_b, keep_a, got_b, got_a = refs[:4]
+    outs = refs[4:]
+    for i in range(3):
+        for shift in range(4):
+            first = (me[5 + i] + shift) % 4 * ROWS
+
+            def step(r, carry, first=first, out=outs[i * 4 + shift]):
+                rows = pl.ds(pl.multiple_of(first + r * 32, 32), 32)
+                to = pl.ds(pl.multiple_of(r * 32, 32), 32)
+                for j, (keep, got) in enumerate(((keep_b, got_b), (keep_a, got_a))):
+                    out[j, to, :] = (keep[i, rows, :].astype(f32) + got[i, rows, :].astype(f32)).astype(bf16)
+                return carry
+
+            lax.fori_loop(0, ROWS // 32, step, 0)
+
+
+def fold_call(me, keep_b, keep_a, got_b, got_a):
+    return pl.pallas_call(
+        fold_kernel,
+        out_shape=[sds((2, ROWS, HALF))] * 12,
+        in_specs=[S] + [V] * 4,
+        out_specs=[V] * 12,
+        name="fold_cores",
+    )(me, keep_b, keep_a, got_b, got_a)
+
+
+def add_kernel(scale, a, b, c, d, out):
+    def step(r, carry):
+        at = (slice(None), pl.ds(pl.multiple_of(r * 32, 32), 32), slice(None))
+        total = (a[at].astype(f32) + c[at].astype(f32)) + (b[at].astype(f32) + d[at].astype(f32))
+        out[at] = (total * scale).astype(bf16)
+        return carry
+
+    lax.fori_loop(0, ROWS // 32, step, 0)
+
+
+def add_call(parts, scale):
+    return pl.pallas_call(
+        lambda *refs: add_kernel(scale, *refs),
+        out_shape=sds((2, ROWS, HALF)),
+        in_specs=[V] * 4,
+        out_specs=V,
+        name="add_ring",
+    )(*parts)
+
+
+def join_kernel(me, *refs):
+    mine, theirs, out, sems = refs[:12], refs[12:24], refs[24], refs[25]
+    for core in range(2):
+        @pl.when(me[2] == core)
+        def _():
+            copies = []
+            for i in range(3):
+                for shift in range(4):
+                    rows = pl.ds(pl.multiple_of((me[5 + i] + 4 - shift) % 4 * ROWS, ROWS), ROWS)
+                    for j in range(2):
+                        k = i * 4 + shift
+                        for n, (half, ref) in enumerate(((core, mine[k]), (1 - core, theirs[k]))):
+                            copies.append(pltpu.make_async_copy(
+                                ref.at[j], out.at[3 * j + i, rows, pl.ds(half * HALF, HALF)],
+                                sems.at[(k * 2 + j) * 2 + n]))
+            for copy in copies:
+                copy.start()
+            for copy in copies:
+                copy.wait()
 
 
 def join_call(me, mine, theirs):
-    half = pl.BlockSpec((1, D, HALF), lambda i, me: (i, 0, 0))
     return pl.pallas_call(
         join_kernel,
         out_shape=sds((6, D, D)),
-        grid_spec=pltpu.PrefetchScalarGridSpec(
-            num_scalar_prefetch=1,
-            grid=(6,),
-            in_specs=[half, half],
-            out_specs=pl.BlockSpec((1, D, D), lambda i, me: (i, 0, 0)),
-        ),
+        in_specs=[S] + [ANY] * 24,
+        out_specs=V,
+        scratch_shapes=[pltpu.SemaphoreType.DMA((48,))],
         name="join_halves",
-    )(me, mine, theirs)
-
-
-CHIPS = ("z", "yl", "x", "yh")
+    )(me, *mine, *theirs)
+
+
+RINGS = (("x",), ("yl", "yh"), ("z",))
+
+
+def ring(matrix, axis, shift):
+    place = (0, 2, 1, 3) if axis == 1 else (0, 1, 2, 3)
+    return lax.ppermute(matrix, RINGS[axis], [(place[i], place[(i + shift) % 4]) for i in range(4)])
 
 
 def exchange(matrix, axes):
@@ -340,11 +379,22 @@
     return lax.ppermute(matrix, "c", [(0, 1), (1, 0)])
 
 
-def reduce_grads(keep, send):
-    half = (keep.astype(f32) + swap_core(send).astype(f32)).astype(bf16)
-    pieces = exchange(half.reshape(64, -1, HALF), CHIPS)
-    total = (jnp.sum(pieces.astype(f32), axis=0) * (1.0 / 256.0)).astype(bf16)
-    return exchange(jnp.broadcast_to(total[None], pieces.shape), CHIPS).reshape(-1, D, HALF)
+def reduce_grads(me, keep_b, keep_a, got_b, got_a):
+    pieces = fold_call(me, keep_b, keep_a, got_b, got_a)
+    totals = []
+    for i in range(3):
+        own = pieces[4 * i:4 * i + 4]
+        totals.append(add_call([own[0]] + [ring(own[n], i, n) for n in range(1, 4)], 1.0))
+    for stage in (1, 2):
+        for i in range(3):
+            got = [ring(totals[i], (i + stage) % 3, n) for n in range(1, 4)]
+            totals[i] = add_call([totals[i]] + got, 1.0 if stage == 1 else 1.0 / 256.0)
+    mine, theirs = [], []
+    for i in range(3):
+        mine += [totals[i]] + [ring(totals[i], i, n) for n in range(1, 4)]
+    for piece in mine:
+        theirs.append(swap_core(piece))
+    return join_call(me, mine, theirs)
 
 
 def layer(
@@ -352,11 +402,11 @@
     pocket_bias, bin_table, bond_weight, w_query, w_key, w_value, w_out, w_cross_query, w_cross_out, cotangent,
 ):
     z, yl, x, yh, c = (lax.axis_index(n) for n in ("z", "yl", "x", "yh", "c"))
-    me = jnp.stack([x, yh, c, z * 2 + yl, x * 4 + yh * 2 + c]).astype(jnp.int32)
+    me = jnp.stack([x, yh, c, z * 2 + yl, x * 4 + yh * 2 + c, x, yh * 2 + yl, z]).astype(jnp.int32)
     note = jnp.concatenate([molecule, jnp.broadcast_to(block_counts, (8, A))], axis=0)
     notes = exchange(jnp.broadcast_to(note[None], (8, 16, A)), ("z", "yl"))
-    packed = pack_call(atoms, distance_bins, bonds)
-    rolled = roll_call(notes, me, packed)
+    codes = jnp.concatenate([distance_bins, bonds], axis=2).astype(bf16)
+    rolled = roll_call(notes, me, atoms, codes)
     got = exchange(rolled, ("z", "yl"))
     pocket = jnp.concatenate(
         [
@@ -390,9 +440,10 @@
         chosen, me, near, far, cq, dc, mid, at, cot, w_cross_out, w_cross_query, w_out
     )
     keep_b, send_b = back_call(me, xs, q, k, v, probs, da)
-    mine = reduce_grads(jnp.concatenate([keep_b, keep_a]), jnp.concatenate([send_b, send_a]))
-    theirs = swap_core(mine)
-    return updated.reshape(cotangent.shape), join_call(me, mine, theirs)
+    got_a = swap_core(send_a)
+    got_b = swap_core(send_b)
+    grads = reduce_grads(me, keep_b, keep_a, got_b, got_a)
+    return updated.reshape(cotangent.shape), grads
 
 
 def solution(mesh):

time: 339 us -> 291 us (0.86); the launches traced: 338 us -> 286 us
  blocking collectives: 98.9 us -> 0 us
  starting transfers between devices: 39.4 us -> 83.6 us
  Pallas kernels: 148 us -> 106 us
  waiting for transfers between devices: 41.2 us -> 83.1 us
  local copies, waits for them, and re-layouts: 4.35 us -> 8.03 us
    all_to_all x2 -> x0, blocking collectives: 98.9 us -> none  [exchange(): return lax.all_to_all(matrix, axes, split_axis=0, concat_axis=0, tiled=True)]
    pallas_call x1, Pallas kernels: 66.5 us -> 4.81 us  [roll_call(): pl.pallas_call(roll_kernel, out_shape=sds((8, A, D + 2 * A)), in_specs=[S...]
    ppermute x0 -> x36, waiting for transfers between devices: none -> 46.4 us  [ring(): lax.ppermute(matrix, RINGS[axis], [(place[i], place[(i + shift) % 4]) for...]
    ppermute x0 -> x36, starting transfers between devices: none -> 39.5 us  [ring(): lax.ppermute(matrix, RINGS[axis], [(place[i], place[(i + shift) % 4]) for...]
    pallas_call x2 -> x11, Pallas kernels: 13.7 us -> 32.8 us  [the longest x9 19.3 us: add_call(): pl.pallas_call(lambda *refs: add_kernel(scale, *refs), out_shape=sds((2,...]
    ppermute x10 -> x22, starting transfers between devices: 17.5 us -> 23.5 us  [swap_core(): return lax.ppermute(matrix, 'c', [(0, 1), (1, 0)])]
    ppermute x10 -> x22, waiting for transfers between devices: 12.2 us -> 7.38 us  [swap_core(): return lax.ppermute(matrix, 'c', [(0, 1), (1, 0)])]
    unnamed x30 -> x120, local copies, waits for them, and re-layouts: 1.97 us -> 6.02 us
  transfers between devices with their start and end apart: 19 -> 67, of which waited for: 4 -> 21; matrix products, arithmetic and copies ran while one was open for 0% -> 2% of each run, Pallas kernels for 8% -> 14%
where the time goes in v3:
time: 291 us; the launch traced here: 286 us
  Pallas kernels  106 us (36%)
  starting transfers between devices  83.6 us (29%)
  waiting for transfers between devices  83.1 us (29%)
  local copies, waits for them, and re-layouts  8.03 us (3%)
  other arithmetic  3.8 us (1%)
    ppermute x36, waiting for transfers between devices, ring(): lax.ppermute(matrix, RINGS[axis], [(place[i], place[(i + shift) % 4]) for...  46.4 us
    ppermute x36, starting transfers between devices, ring(): lax.ppermute(matrix, RINGS[axis], [(place[i], place[(i + shift) % 4]) for...  39.5 us
    pallas_call x1, Pallas kernels, cross_call(): pl.pallas_call(cross_kernel, out_shape=[sds((R, D)), sds((R, D)), sds((3,...  31.8 us
    ppermute x7, waiting for transfers between devices, shifted(): return lax.ppermute(matrix, ('x', 'yh'), pairs)  27.8 us
    ppermute x22, starting transfers between devices, swap_core(): return lax.ppermute(matrix, 'c', [(0, 1), (1, 0)])  23.5 us
    pallas_call x9, Pallas kernels, add_call(): pl.pallas_call(lambda *refs: add_kernel(scale, *refs), out_shape=sds((2,...  19.3 us
    pallas_call x1, Pallas kernels, back_call(): pl.pallas_call(back_kernel, out_shape=[sds((3, D, HALF)), sds((3, D, HALF...  16.1 us
    pallas_call x1, Pallas kernels, self_call(): pl.pallas_call(self_kernel, out_shape=[sds((R, D)) for _ in range(4)] + [...  15.5 us
  transfers between devices with their start and end apart: 67, of which 21 were waited for; matrix products, arithmetic and copies ran while one was open for 2% of the time, Pallas kernels for 14%

profile of v3, /device:TPU:1, one launch (start us, length us, event | category | flops | bytes accessed | tf_op | source)
XLA Modules:
  0.0 286.2 jit_solution(14404978849891800966)
XLA Ops:
  2.6 6.9 %all-to-all-start = ((s32[8,16,128]{2,1,0:T(8,128)}), s32[8,16,128]{2,1,0:T(8,128)S(1)}, u32[]{:S(2)}, u32[]{:S(2)}) async-start(s32[8,16,128]{2,1,0:T(8,128)} %broadcast_in_dim.11), calls=%async_computation | async-start | bytes 131072 | tf_op jit(solution)/shard_map/all_to_all | solution.py:367
  15.3 4.8 %roll_slots.1 = bf16[8,128,1024]{2,1,0:T(8,128)(2,1)} custom-call(s32[8,16,128]{2,1,0:T(8,128)} %copy-done.3, s32[8]{0:T(128)} %stack.32.me, bf16[8,128,768]{2,1,0:T(8,128)(2,1)} %atoms.1, bf16[8,128,256]{2,1,0:T(8,128)(2,1)} %pad_maximum_fusion.codes), custom_call_target="tpu_custom_call" | custom-call | tf_op jit(solution)/shard_map/roll_slots/pallas_call | solution.py:241
  20.2 3.7 %all-to-all-start.1 = ((bf16[8,128,1024]{2,1,0:T(8,128)(2,1)}), bf16[8,128,1024]{2,1,0:T(8,128)(2,1)S(1)}, u32[]{:S(2)}, u32[]{:S(2)}) async-start(bf16[8,128,1024]{2,1,0:T(8,128)(2,1)} %roll_slots.1), calls=%async_computation.1 | async-start | bytes 4194304 | tf_op jit(solution)/shard_map/all_to_all | solution.py:367
  24.0 2.7 collective-permute-start
  26.7 2.4 collective-permute-start.7
  29.1 2.5 collective-permute-start.5
  32.8 24.5 %collective-permute-done.refs_1_ = bf16[136,1536]{1,0:T(8,128)(2,1)S(1)} collective-permute-done((bf16[136,1536]{1,0:T(8,128)(2,1)S(1)}, bf16[136,1536]{1,0:T(8,128)(2,1)S(1)}, u32[]{:S(2)}, u32[]{:S(2)}) %collective-permute-start) | collective-permute-done | bytes 417824 | tf_op jit(solution)/shard_map/ppermute | solution.py:375
  57.3 2.5 collective-permute-start.6
  60.9 3.5 %collective-permute-start.13 = (bf16[136,1536]{1,0:T(8,128)(2,1)}, bf16[136,1536]{1,0:T(8,128)(2,1)}, u32[]{:S(2)}, u32[]{:S(2)}) collective-permute-start(bf16[136,1536]{1,0:T(8,128)(2,1)} %collective-permute-done.5.refs_6_), channel_id=1, source_target_pairs={{0,1},{1,0},{2,3},{3,2},{4,5},{5,4},{6,7},{7,6},{8,9},{9,8},{10,11... | collective-permute-start | bytes 1253384 | tf_op jit(solution)/shard_map/ppermute | solution.py:379
  65.9 4.6 %find_blocks.1 = (s32[4]{0:T(128)}, s32[4]{0:T(128)}, s32[16]{0:T(128)}) custom-call(s32[8,16,128]{2,1,0:T(8,128)} %copy-done.3, s32[8]{0:T(128)} %stack.32.me, s32[1024]{0:T(1024)} %scaffold.1, s32[4,8192]{1,0:T(4,128)} %bitcast.13), custom_call_target="tpu_custom_call" | custom-call | tf_op jit(solution)/shard_map/find_blocks/pallas_call | solution.py:270
  71.2 7.4 %collective-permute-start.14 = (bf16[136,1536]{1,0:T(8,128)(2,1)}, bf16[136,1536]{1,0:T(8,128)(2,1)}, u32[]{:S(2)}, u32[]{:S(2)}) collective-permute-start(bf16[136,1536]{1,0:T(8,128)(2,1)} %collective-permute-done.6.refs_7_), channel_id=1, source_target_pairs={{0,1},{1,0},{2,3},{3,2},{4,5},{5,4},{6,7},{7,6},{8,9},{9,8},{10,11... | collective-permute-start | bytes 1253384 | tf_op jit(solution)/shard_map/ppermute | solution.py:379
  78.6 3.3 %collective-permute-done.2.refs_3_ = bf16[136,1536]{1,0:T(8,128)(2,1)} collective-permute-done((bf16[136,1536]{1,0:T(8,128)(2,1)S(1)}, bf16[136,1536]{1,0:T(8,128)(2,1)}, u32[]{:S(2)}, u32[]{:S(2)}) %collective-permute-start.2) | collective-permute-done | bytes 417824 | tf_op jit(solution)/shard_map/ppermute | solution.py:375
  84.1 15.5 %self_forward.1 = (bf16[512,768]{1,0:T(8,128)(2,1)}, bf16[512,768]{1,0:T(8,128)(2,1)}, bf16[512,768]{1,0:T(8,128)(2,1)}, bf16[512,768]{1,0:T(8,128)(2,1)}, f32[4...) custom-call(s32[4]{0:T(128)} %get-tuple-element.33.src, ...), custom_call_target="tpu_custom_call" | custom-call | flops 16000000000 | bytes 8000000 | tf_op jit(solution)/shard_map/self_forward/pallas_call | solution.py:188
  99.8 31.8 %cross_both.1 = (bf16[512,768]{1,0:T(8,128)(2,1)}, bf16[512,768]{1,0:T(8,128)(2,1)}, bf16[3,768,384]{2,1,0:T(8,128)(2,1)}, bf16[3,768,384]{2,1,0:T(8,128)(2,1)}) custom-call(s32[16]{0:T(128)} %get-tuple-element.32.chosen, s32[8]{0:T(128)} %stack.32.me, bf16[136,1536]{1,0:T(8,128)(2,1)} %copy-done.4, bf16[136,1536]{1,0:T(8,128)(2,1)} %copy-done.57, ...), custom_call_target="tpu_custom_call" | custom-call | flops 28000000000 | bytes 8000000 | tf_op jit(solution)/shard_map/cross_both/pallas_call | solution.py:201
  131.6 16.1 %self_backward.1 = (bf16[3,768,384]{2,1,0:T(8,128)(2,1)}, bf16[3,768,384]{2,1,0:T(8,128)(2,1)}) custom-call(s32[8]{0:T(128)} %stack.32.me, bf16[512,768]{1,0:T(8,128)(2,1)} %get-tuple-element.40.x, bf16[512,768]{1,0:T(8,128)(2,1)} %get-tuple-element.41.q, bf16[512,768]{1,0:T(8,128)(2,1)} %get-tuple-element.42.k, bf16[512,768]{1,0:T(8,128)(2,1)} %get-tuple-element.43.v, ...), custom_call_target="tpu_custom_call" | custom-call | flops 16000000000 | bytes 8000000 | tf_op jit(solution)/shard_map/self_backward/pallas_call | solution.py:214
  148.2 3.4 %collective-permute-done.15.refs_2_ = bf16[3,768,384]{2,1,0:T(8,128)(2,1)S(1)} collective-permute-done((bf16[3,768,384]{2,1,0:T(8,128)(2,1)}, bf16[3,768,384]{2,1,0:T(8,128)(2,1)S(1)}, u32[]{:S(2)}, u32[]{:S(2)}) %collective-permute-start.15) | collective-permute-done | bytes 1769504 | tf_op jit(solution)/shard_map/ppermute | solution.py:379
  151.6 2.5 collective-permute-done.16.refs_3_
  155.4 6.3 %fold_cores.1 = (bf16[2,192,384]{2,1,0:T(8,128)(2,1)}, bf16[2,192,384]{2,1,0:T(8,128)(2,1)}, bf16[2,192,384]{2,1,0:T(8,128)(2,1)}, bf16[2,192,384]{2,1,0:T(8,128...) custom-call(s32[8]{0:T(128)} %stack.32.me, ...), custom_call_target="tpu_custom_call" | custom-call | tf_op jit(solution)/shard_map/fold_cores/pallas_call | solution.py:297
  166.4 11.4 %collective-permute-done.17.refs_1_ = bf16[2,192,384]{2,1,0:T(8,128)(2,1)S(1)} collective-permute-done((bf16[2,192,384]{2,1,0:T(8,128)(2,1)}, bf16[2,192,384]{2,1,0:T(8,128)(2,1)S(1)}, u32[]{:S(2)}, u32[]{:S(2)}) %collective-permute-start.17) | collective-permute-done | bytes 294944 | tf_op jit(solution)/shard_map/ppermute | solution.py:363
  180.0 2.4 collective-permute-start.42
  183.5 2.1 add_ring.9.refs_0_
  185.7 2.4 collective-permute-start.21
  188.1 2.1 add_ring.12.refs_0_
  190.5 4.2 %collective-permute-done.42.refs_2_ = bf16[2,192,384]{2,1,0:T(8,128)(2,1)S(1)} collective-permute-done((bf16[2,192,384]{2,1,0:T(8,128)(2,1)}, bf16[2,192,384]{2,1,0:T(8,128)(2,1)S(1)}, u32[]{:S(2)}, u32[]{:S(2)}) %collective-permute-start.42) | collective-permute-done | bytes 294944 | tf_op jit(solution)/shard_map/ppermute | solution.py:363
  195.1 1.7 collective-permute-start.33
  196.8 2.1 add_ring.15.refs_0_
  199.0 2.1 collective-permute-start.32
  204.5 2.1 add_ring.10.refs_0_
  206.7 3.4 %collective-permute-start.25 = (bf16[2,192,384]{2,1,0:T(8,128)(2,1)}, bf16[2,192,384]{2,1,0:T(8,128)(2,1)S(1)}, u32[]{:S(2)}, u32[]{:S(2)}) collective-permute-start(bf16[2,192,384]{2,1,0:T(8,128)(2,1)} %add_ring.10.refs_0_), channel_id=1, source_target_pairs={{0,96},{32,0},{64,32},{96,64},{1,97},{33,1},{65,33},{97,65},{2,98}... | collective-permute-start | bytes 884744 | tf_op jit(solution)/shard_map/ppermute | solution.py:363
  210.8 2.6 collective-permute-start.24
  213.4 2.2 add_ring.13.refs_0_
  215.7 1.8 collective-permute-start.37
  217.5 2.3 collective-permute-done.44.refs_1_
  220.4 2.1 add_ring.16.refs_0_
  223.6 2.9 %collective-permute-done.23.refs_1_ = bf16[2,192,384]{2,1,0:T(8,128)(2,1)S(1)} collective-permute-done((bf16[2,192,384]{2,1,0:T(8,128)(2,1)}, bf16[2,192,384]{2,1,0:T(8,128)(2,1)S(1)}, u32[]{:S(2)}, u32[]{:S(2)}) %collective-permute-start.23) | collective-permute-done | bytes 294944 | tf_op jit(solution)/shard_map/ppermute | solution.py:363
  226.5 2.4 collective-permute-start.48
  229.0 2.1 add_ring.11.refs_0_
  231.1 2.9 %collective-permute-start.53 = (bf16[2,192,384]{2,1,0:T(8,128)(2,1)}, bf16[2,192,384]{2,1,0:T(8,128)(2,1)S(1)}, u32[]{:S(2)}, u32[]{:S(2)}) collective-permute-start(bf16[2,192,384]{2,1,0:T(8,128)(2,1)} %add_ring.11.refs_0_), channel_id=1, source_target_pairs={{0,1},{1,0},{2,3},{3,2},{4,5},{5,4},{6,7},{7,6},{8,9},{9,8},{10,11... | collective-permute-start | bytes 884744 | tf_op jit(solution)/shard_map/ppermute | solution.py:379
  235.9 2.1 add_ring.14.refs_4_
  239.3 3.6 %collective-permute-done.47.refs_1_ = bf16[2,192,384]{2,1,0:T(8,128)(2,1)S(1)} collective-permute-done((bf16[2,192,384]{2,1,0:T(8,128)(2,1)}, bf16[2,192,384]{2,1,0:T(8,128)(2,1)S(1)}, u32[]{:S(2)}, u32[]{:S(2)}) %collective-permute-start.47) | collective-permute-done | bytes 294944 | tf_op jit(solution)/shard_map/ppermute | solution.py:363
  244.3 2.2 add_ring.17.refs_8_
  246.4 2.5 collective-permute-start.39
  249.4 5.6 %collective-permute-done.26.refs_1_ = bf16[2,192,384]{2,1,0:T(8,128)(2,1)S(1)} collective-permute-done((bf16[2,192,384]{2,1,0:T(8,128)(2,1)}, bf16[2,192,384]{2,1,0:T(8,128)(2,1)S(1)}, u32[]{:S(2)}, u32[]{:S(2)}) %collective-permute-start.26) | collective-permute-done | bytes 294944 | tf_op jit(solution)/shard_map/ppermute | solution.py:363
  255.6 2.3 collective-permute-start.52
  258.5 4.7 %collective-permute-done.38.refs_5_ = bf16[2,192,384]{2,1,0:T(8,128)(2,1)S(1)} collective-permute-done((bf16[2,192,384]{2,1,0:T(8,128)(2,1)}, bf16[2,192,384]{2,1,0:T(8,128)(2,1)S(1)}, u32[]{:S(2)}, u32[]{:S(2)}) %collective-permute-start.38) | collective-permute-done | bytes 294944 | tf_op jit(solution)/shard_map/ppermute | solution.py:363
  264.0 6.6 %collective-permute-done.52.refs_11_ = bf16[2,192,384]{2,1,0:T(8,128)(2,1)S(1)} collective-permute-done((bf16[2,192,384]{2,1,0:T(8,128)(2,1)}, bf16[2,192,384]{2,1,0:T(8,128)(2,1)S(1)}, u32[]{:S(2)}, u32[]{:S(2)}) %collective-permute-start.52) | collective-permute-done | bytes 294944 | tf_op jit(solution)/shard_map/ppermute | solution.py:363
  271.8 2.6 collective-permute-done.50.refs_9_
  278.7 7.2 %join_halves.1 = bf16[6,768,768]{2,1,0:T(8,128)(2,1)} custom-call(s32[8]{0:T(128)} %stack.32.me, bf16[2,192,384]{2,1,0:T(8,128)(2,1)} %add_ring.11.refs_0_, bf16[2,192,384]{2,1,0:T(8,128)(2,1)} %copy-done.8, bf16[2,192,384]{2,1,0:T(8,128)(2,1)} %copy-done.7, bf16[2,192,384]{2,1,0:T(8,128)(2,1)} %copy-done.6, bf16[2,192,384]{2,1,0:T(8,128)(2,1)} %add_ring.14.refs_4_, ...), custom_call_target="tpu_custom_call" | custom-call | tf_op jit(solution)/shard_map/join_halves/pallas_call | solution.py:348
  (234 shorter events, 42.8 us)
Async XLA Ops:
  2.6 12.1 %all-to-all-start = ((s32[8,16,128]{2,1,0:T(8,128)}), s32[8,16,128]{2,1,0:T(8,128)S(1)}, u32[]{:S(2)}, u32[]{:S(2)}) async-start(s32[8,16,128]{2,1,0:T(8,128)} %broadcast_in_dim.11), calls=%async_computation | async-start | bytes 131072 | tf_op jit(solution)/shard_map/all_to_all | solution.py:367
  20.2 62.6 %all-to-all-start.1 = ((bf16[8,128,1024]{2,1,0:T(8,128)(2,1)}), bf16[8,128,1024]{2,1,0:T(8,128)(2,1)S(1)}, u32[]{:S(2)}, u32[]{:S(2)}) async-start(bf16[8,128,1024]{2,1,0:T(8,128)(2,1)} %roll_slots.1), calls=%async_computation.1 | async-start | bytes 4194304 | tf_op jit(solution)/shard_map/all_to_all | solution.py:367
  24.0 33.2 %collective-permute-start = (bf16[136,1536]{1,0:T(8,128)(2,1)S(1)}, bf16[136,1536]{1,0:T(8,128)(2,1)S(1)}, u32[]{:S(2)}, u32[]{:S(2)}) collective-permute-start(bf16[136,1536]{1,0:T(8,128)(2,1)S(1)} %pad_maximum_fusion.1.refs_0_), channel_id=1, source_target_pairs={{0,2},{2,0},{4,6},{6,4},{8,10},{10,8},{12,14},{14,12},{1,3},{3,1},... | collective-permute-start | bytes 1253384 | tf_op jit(solution)/shard_map/ppermute | solution.py:375
  26.7 33.0 %collective-permute-start.7 = (bf16[136,1536]{1,0:T(8,128)(2,1)S(1)}, bf16[136,1536]{1,0:T(8,128)(2,1)S(1)}, u32[]{:S(2)}, u32[]{:S(2)}) collective-permute-start(bf16[136,1536]{1,0:T(8,128)(2,1)S(1)} %pad_maximum_fusion.1.refs_0_), channel_id=1, source_target_pairs={{0,1},{1,0},{2,3},{3,2},{4,5},{5,4},{6,7},{7,6},{8,9},{9,8},{10,11... | collective-permute-start | bytes 1253384 | tf_op jit(solution)/shard_map/ppermute | solution.py:379
  29.1 31.2 %collective-permute-start.5 = (bf16[136,1536]{1,0:T(8,128)(2,1)S(1)}, bf16[136,1536]{1,0:T(8,128)(2,1)}, u32[]{:S(2)}, u32[]{:S(2)}) collective-permute-start(bf16[136,1536]{1,0:T(8,128)(2,1)S(1)} %pad_maximum_fusion.1.refs_0_), channel_id=1, source_target_pairs={{0,12},{2,14},{4,0},{6,2},{8,4},{10,6},{12,8},{14,10},{1,13},{3,15... | collective-permute-start | bytes 1253384 | tf_op jit(solution)/shard_map/ppermute | solution.py:375
  31.6 29.3 %collective-permute-start.3 = (bf16[136,1536]{1,0:T(8,128)(2,1)S(1)}, bf16[136,1536]{1,0:T(8,128)(2,1)}, u32[]{:S(2)}, u32[]{:S(2)}) collective-permute-start(bf16[136,1536]{1,0:T(8,128)(2,1)S(1)} %pad_maximum_fusion.1.refs_0_), channel_id=1, source_target_pairs={{0,8},{2,10},{4,12},{6,14},{8,0},{10,2},{12,4},{14,6},{1,9},{3,11}... | collective-permute-start | bytes 1253384 | tf_op jit(solution)/shard_map/ppermute | solution.py:375
  32.1 32.2 %collective-permute-start.1 = (bf16[136,1536]{1,0:T(8,128)(2,1)S(1)}, bf16[136,1536]{1,0:T(8,128)(2,1)S(1)}, u32[]{:S(2)}, u32[]{:S(2)}) collective-permute-start(bf16[136,1536]{1,0:T(8,128)(2,1)S(1)} %pad_maximum_fusion.1.refs_0_), channel_id=1, source_target_pairs={{0,4},{2,6},{4,8},{6,10},{8,12},{10,14},{12,0},{14,2},{1,5},{3,7},... | collective-permute-start | bytes 1253384 | tf_op jit(solution)/shard_map/ppermute | solution.py:375
  57.3 13.9 %collective-permute-start.6 = (bf16[136,1536]{1,0:T(8,128)(2,1)S(1)}, bf16[136,1536]{1,0:T(8,128)(2,1)}, u32[]{:S(2)}, u32[]{:S(2)}) collective-permute-start(bf16[136,1536]{1,0:T(8,128)(2,1)S(1)} %collective-permute-done.refs_1_), channel_id=1, source_target_pairs={{0,12},{2,14},{4,0},{6,2},{8,4},{10,6},{12,8},{14,10},{1,13},{3,15... | collective-permute-start | bytes 1253384 | tf_op jit(solution)/shard_map/ppermute | solution.py:375
  59.7 18.8 %collective-permute-start.4 = (bf16[136,1536]{1,0:T(8,128)(2,1)S(1)}, bf16[136,1536]{1,0:T(8,128)(2,1)}, u32[]{:S(2)}, u32[]{:S(2)}) collective-permute-start(bf16[136,1536]{1,0:T(8,128)(2,1)S(1)} %collective-permute-done.refs_1_), channel_id=1, source_target_pairs={{0,8},{2,10},{4,12},{6,14},{8,0},{10,2},{12,4},{14,6},{1,9},{3,11}... | collective-permute-start | bytes 1253384 | tf_op jit(solution)/shard_map/ppermute | solution.py:375
  60.3 21.6 %collective-permute-start.2 = (bf16[136,1536]{1,0:T(8,128)(2,1)S(1)}, bf16[136,1536]{1,0:T(8,128)(2,1)}, u32[]{:S(2)}, u32[]{:S(2)}) collective-permute-start(bf16[136,1536]{1,0:T(8,128)(2,1)S(1)} %collective-permute-done.refs_1_), channel_id=1, source_target_pairs={{0,4},{2,6},{4,8},{6,10},{8,12},{10,14},{12,0},{14,2},{1,5},{3,7},... | collective-permute-start | bytes 1253384 | tf_op jit(solution)/shard_map/ppermute | solution.py:375
  70.5 29.2 %collective-permute-start.8 = (bf16[136,1536]{1,0:T(8,128)(2,1)S(1)}, bf16[136,1536]{1,0:T(8,128)(2,1)}, u32[]{:S(2)}, u32[]{:S(2)}) collective-permute-start(bf16[136,1536]{1,0:T(8,128)(2,1)S(1)} %collective-permute-done.refs_1_), channel_id=1, source_target_pairs={{0,1},{1,0},{2,3},{3,2},{4,5},{5,4},{6,7},{7,6},{8,9},{9,8},{10,11... | collective-permute-start | bytes 1253384 | tf_op jit(solution)/shard_map/ppermute | solution.py:379
  71.1 28.6 %collective-permute-start.9 = (bf16[136,1536]{1,0:T(8,128)(2,1)}, bf16[136,1536]{1,0:T(8,128)(2,1)}, u32[]{:S(2)}, u32[]{:S(2)}) collective-permute-start(bf16[136,1536]{1,0:T(8,128)(2,1)} %copy-done.59), channel_id=1, source_target_pairs={{0,1},{1,0},{2,3},{3,2},{4,5},{5,4},{6,7},{7,6},{8,9},{9,8},{10,11... | collective-permute-start | bytes 1253384 | tf_op jit(solution)/shard_map/ppermute | solution.py:379
  71.2 28.6 %collective-permute-start.14 = (bf16[136,1536]{1,0:T(8,128)(2,1)}, bf16[136,1536]{1,0:T(8,128)(2,1)}, u32[]{:S(2)}, u32[]{:S(2)}) collective-permute-start(bf16[136,1536]{1,0:T(8,128)(2,1)} %collective-permute-done.6.refs_7_), channel_id=1, source_target_pairs={{0,1},{1,0},{2,3},{3,2},{4,5},{5,4},{6,7},{7,6},{8,9},{9,8},{10,11... | collective-permute-start | bytes 1253384 | tf_op jit(solution)/shard_map/ppermute | solution.py:379
  78.6 21.2 %collective-permute-start.12 = (bf16[136,1536]{1,0:T(8,128)(2,1)}, bf16[136,1536]{1,0:T(8,128)(2,1)}, u32[]{:S(2)}, u32[]{:S(2)}) collective-permute-start(bf16[136,1536]{1,0:T(8,128)(2,1)} %collective-permute-done.4.refs_5_), channel_id=1, source_target_pairs={{0,1},{1,0},{2,3},{3,2},{4,5},{5,4},{6,7},{7,6},{8,9},{9,8},{10,11... | collective-permute-start | bytes 1253384 | tf_op jit(solution)/shard_map/ppermute | solution.py:379
  81.9 17.9 %collective-permute-start.10 = (bf16[136,1536]{1,0:T(8,128)(2,1)}, bf16[136,1536]{1,0:T(8,128)(2,1)}, u32[]{:S(2)}, u32[]{:S(2)}) collective-permute-start(bf16[136,1536]{1,0:T(8,128)(2,1)} %collective-permute-done.2.refs_3_), channel_id=1, source_target_pairs={{0,1},{1,0},{2,3},{3,2},{4,5},{5,4},{6,7},{7,6},{8,9},{9,8},{10,11... | collective-permute-start | bytes 1253384 | tf_op jit(solution)/shard_map/ppermute | solution.py:379
  161.7 16.2 %collective-permute-start.17 = (bf16[2,192,384]{2,1,0:T(8,128)(2,1)}, bf16[2,192,384]{2,1,0:T(8,128)(2,1)S(1)}, u32[]{:S(2)}, u32[]{:S(2)}) collective-permute-start(bf16[2,192,384]{2,1,0:T(8,128)(2,1)} %get-tuple-element.51), channel_id=1, source_target_pairs={{0,4},{4,8},{8,12},{12,0},{1,5},{5,9},{9,13},{13,1},{2,6},{6,10},{... | collective-permute-start | bytes 884744 | tf_op jit(solution)/shard_map/ppermute | solution.py:363
  161.7 17.1 %collective-permute-start.18 = (bf16[2,192,384]{2,1,0:T(8,128)(2,1)}, bf16[2,192,384]{2,1,0:T(8,128)(2,1)S(1)}, u32[]{:S(2)}, u32[]{:S(2)}) collective-permute-start(bf16[2,192,384]{2,1,0:T(8,128)(2,1)} %get-tuple-element.52), channel_id=1, source_target_pairs={{0,8},{4,12},{8,0},{12,4},{1,9},{5,13},{9,1},{13,5},{2,10},{6,14},... | collective-permute-start | bytes 884744 | tf_op jit(solution)/shard_map/ppermute | solution.py:363
  163.2 16.8 %collective-permute-start.19 = (bf16[2,192,384]{2,1,0:T(8,128)(2,1)}, bf16[2,192,384]{2,1,0:T(8,128)(2,1)S(1)}, u32[]{:S(2)}, u32[]{:S(2)}) collective-permute-start(bf16[2,192,384]{2,1,0:T(8,128)(2,1)} %get-tuple-element.53), channel_id=1, source_target_pairs={{0,12},{4,0},{8,4},{12,8},{1,13},{5,1},{9,5},{13,9},{2,14},{6,2},{... | collective-permute-start | bytes 884744 | tf_op jit(solution)/shard_map/ppermute | solution.py:363
  164.4 18.0 %collective-permute-start.29 = (bf16[2,192,384]{2,1,0:T(8,128)(2,1)}, bf16[2,192,384]{2,1,0:T(8,128)(2,1)S(1)}, u32[]{:S(2)}, u32[]{:S(2)}) collective-permute-start(bf16[2,192,384]{2,1,0:T(8,128)(2,1)} %get-tuple-element.55), channel_id=1, source_target_pairs={{0,16},{16,2},{2,18},{18,0},{1,17},{17,3},{3,19},{19,1},{4,20},{20... | collective-permute-start | bytes 884744 | tf_op jit(solution)/shard_map/ppermute | solution.py:363
  164.9 20.7 %collective-permute-start.30 = (bf16[2,192,384]{2,1,0:T(8,128)(2,1)}, bf16[2,192,384]{2,1,0:T(8,128)(2,1)S(1)}, u32[]{:S(2)}, u32[]{:S(2)}) collective-permute-start(bf16[2,192,384]{2,1,0:T(8,128)(2,1)} %get-tuple-element.56), channel_id=1, source_target_pairs={{0,2},{16,18},{2,0},{18,16},{1,3},{17,19},{3,1},{19,17},{4,6},{20,... | collective-permute-start | bytes 884744 | tf_op jit(solution)/shard_map/ppermute | solution.py:363
  178.7 11.5 %collective-permute-start.41 = (bf16[2,192,384]{2,1,0:T(8,128)(2,1)}, bf16[2,192,384]{2,1,0:T(8,128)(2,1)S(1)}, u32[]{:S(2)}, u32[]{:S(2)}) collective-permute-start(bf16[2,192,384]{2,1,0:T(8,128)(2,1)} %get-tuple-element.59), channel_id=1, source_target_pairs={{0,32},{32,64},{64,96},{96,0},{1,33},{33,65},{65,97},{97,1},{2,34}... | collective-permute-start | bytes 884744 | tf_op jit(solution)/shard_map/ppermute | solution.py:363
  180.0 14.7 %collective-permute-start.42 = (bf16[2,192,384]{2,1,0:T(8,128)(2,1)}, bf16[2,192,384]{2,1,0:T(8,128)(2,1)S(1)}, u32[]{:S(2)}, u32[]{:S(2)}) collective-permute-start(bf16[2,192,384]{2,1,0:T(8,128)(2,1)} %get-tuple-element.60), channel_id=1, source_target_pairs={{0,64},{32,96},{64,0},{96,32},{1,65},{33,97},{65,1},{97,33},{2,66}... | collective-permute-start | bytes 884744 | tf_op jit(solution)/shard_map/ppermute | solution.py:363
  182.3 12.8 %collective-permute-start.43 = (bf16[2,192,384]{2,1,0:T(8,128)(2,1)}, bf16[2,192,384]{2,1,0:T(8,128)(2,1)S(1)}, u32[]{:S(2)}, u32[]{:S(2)}) collective-permute-start(bf16[2,192,384]{2,1,0:T(8,128)(2,1)} %get-tuple-element.61), channel_id=1, source_target_pairs={{0,96},{32,0},{64,32},{96,64},{1,97},{33,1},{65,33},{97,65},{2,98}... | collective-permute-start | bytes 884744 | tf_op jit(solution)/shard_map/ppermute | solution.py:363
  185.6 13.3 %collective-permute-start.22 = (bf16[2,192,384]{2,1,0:T(8,128)(2,1)}, bf16[2,192,384]{2,1,0:T(8,128)(2,1)S(1)}, u32[]{:S(2)}, u32[]{:S(2)}) collective-permute-start(bf16[2,192,384]{2,1,0:T(8,128)(2,1)} %add_ring.9.refs_0_), channel_id=1, source_target_pairs={{0,18},{16,0},{2,16},{18,2},{1,19},{17,1},{3,17},{19,3},{4,22},{20... | collective-permute-start | bytes 884744 | tf_op jit(solution)/shard_map/ppermute | solution.py:363
  185.7 15.4 %collective-permute-start.21 = (bf16[2,192,384]{2,1,0:T(8,128)(2,1)}, bf16[2,192,384]{2,1,0:T(8,128)(2,1)S(1)}, u32[]{:S(2)}, u32[]{:S(2)}) collective-permute-start(bf16[2,192,384]{2,1,0:T(8,128)(2,1)} %add_ring.9.refs_0_), channel_id=1, source_target_pairs={{0,2},{16,18},{2,0},{18,16},{1,3},{17,19},{3,1},{19,17},{4,6},{20,... | collective-permute-start | bytes 884744 | tf_op jit(solution)/shard_map/ppermute | solution.py:363
  190.2 12.6 %collective-permute-start.20 = (bf16[2,192,384]{2,1,0:T(8,128)(2,1)}, bf16[2,192,384]{2,1,0:T(8,128)(2,1)S(1)}, u32[]{:S(2)}, u32[]{:S(2)}) collective-permute-start(bf16[2,192,384]{2,1,0:T(8,128)(2,1)} %add_ring.9.refs_0_), channel_id=1, source_target_pairs={{0,16},{16,2},{2,18},{18,0},{1,17},{17,3},{3,19},{19,1},{4,20},{20... | collective-permute-start | bytes 884744 | tf_op jit(solution)/shard_map/ppermute | solution.py:363
  195.1 11.6 %collective-permute-start.33 = (bf16[2,192,384]{2,1,0:T(8,128)(2,1)}, bf16[2,192,384]{2,1,0:T(8,128)(2,1)S(1)}, u32[]{:S(2)}, u32[]{:S(2)}) collective-permute-start(bf16[2,192,384]{2,1,0:T(8,128)(2,1)} %add_ring.12.refs_0_), channel_id=1, source_target_pairs={{0,64},{32,96},{64,0},{96,32},{1,65},{33,97},{65,1},{97,33},{2,66}... | collective-permute-start | bytes 884744 | tf_op jit(solution)/shard_map/ppermute | solution.py:363
  199.0 11.8 %collective-permute-start.32 = (bf16[2,192,384]{2,1,0:T(8,128)(2,1)}, bf16[2,192,384]{2,1,0:T(8,128)(2,1)S(1)}, u32[]{:S(2)}, u32[]{:S(2)}) collective-permute-start(bf16[2,192,384]{2,1,0:T(8,128)(2,1)} %add_ring.12.refs_0_), channel_id=1, source_target_pairs={{0,32},{32,64},{64,96},{96,0},{1,33},{33,65},{65,97},{97,1},{2,34}... | collective-permute-start | bytes 884744 | tf_op jit(solution)/shard_map/ppermute | solution.py:363
  201.1 12.3 %collective-permute-start.46 = (bf16[2,192,384]{2,1,0:T(8,128)(2,1)}, bf16[2,192,384]{2,1,0:T(8,128)(2,1)S(1)}, u32[]{:S(2)}, u32[]{:S(2)}) collective-permute-start(bf16[2,192,384]{2,1,0:T(8,128)(2,1)} %add_ring.15.refs_0_), channel_id=1, source_target_pairs={{0,12},{4,0},{8,4},{12,8},{1,13},{5,1},{9,5},{13,9},{2,14},{6,2},{... | collective-permute-start | bytes 884744 | tf_op jit(solution)/shard_map/ppermute | solution.py:363
  202.8 12.9 %collective-permute-start.45 = (bf16[2,192,384]{2,1,0:T(8,128)(2,1)}, bf16[2,192,384]{2,1,0:T(8,128)(2,1)S(1)}, u32[]{:S(2)}, u32[]{:S(2)}) collective-permute-start(bf16[2,192,384]{2,1,0:T(8,128)(2,1)} %add_ring.15.refs_0_), channel_id=1, source_target_pairs={{0,8},{4,12},{8,0},{12,4},{1,9},{5,13},{9,1},{13,5},{2,10},{6,14},... | collective-permute-start | bytes 884744 | tf_op jit(solution)/shard_map/ppermute | solution.py:363
  202.8 16.9 %collective-permute-start.44 = (bf16[2,192,384]{2,1,0:T(8,128)(2,1)}, bf16[2,192,384]{2,1,0:T(8,128)(2,1)S(1)}, u32[]{:S(2)}, u32[]{:S(2)}) collective-permute-start(bf16[2,192,384]{2,1,0:T(8,128)(2,1)} %add_ring.15.refs_0_), channel_id=1, source_target_pairs={{0,4},{4,8},{8,12},{12,0},{1,5},{5,9},{9,13},{13,1},{2,6},{6,10},{... | collective-permute-start | bytes 884744 | tf_op jit(solution)/shard_map/ppermute | solution.py:363
  206.7 15.9 %collective-permute-start.25 = (bf16[2,192,384]{2,1,0:T(8,128)(2,1)}, bf16[2,192,384]{2,1,0:T(8,128)(2,1)S(1)}, u32[]{:S(2)}, u32[]{:S(2)}) collective-permute-start(bf16[2,192,384]{2,1,0:T(8,128)(2,1)} %add_ring.10.refs_0_), channel_id=1, source_target_pairs={{0,96},{32,0},{64,32},{96,64},{1,97},{33,1},{65,33},{97,65},{2,98}... | collective-permute-start | bytes 884744 | tf_op jit(solution)/shard_map/ppermute | solution.py:363
  210.8 11.8 %collective-permute-start.24 = (bf16[2,192,384]{2,1,0:T(8,128)(2,1)}, bf16[2,192,384]{2,1,0:T(8,128)(2,1)S(1)}, u32[]{:S(2)}, u32[]{:S(2)}) collective-permute-start(bf16[2,192,384]{2,1,0:T(8,128)(2,1)} %add_ring.10.refs_0_), channel_id=1, source_target_pairs={{0,64},{32,96},{64,0},{96,32},{1,65},{33,97},{65,1},{97,33},{2,66}... | collective-permute-start | bytes 884744 | tf_op jit(solution)/shard_map/ppermute | solution.py:363
  213.4 13.1 %collective-permute-start.23 = (bf16[2,192,384]{2,1,0:T(8,128)(2,1)}, bf16[2,192,384]{2,1,0:T(8,128)(2,1)S(1)}, u32[]{:S(2)}, u32[]{:S(2)}) collective-permute-start(bf16[2,192,384]{2,1,0:T(8,128)(2,1)} %add_ring.10.refs_0_), channel_id=1, source_target_pairs={{0,32},{32,64},{64,96},{96,0},{1,33},{33,65},{65,97},{97,1},{2,34}... | collective-permute-start | bytes 884744 | tf_op jit(solution)/shard_map/ppermute | solution.py:363
  215.7 15.4 %collective-permute-start.37 = (bf16[2,192,384]{2,1,0:T(8,128)(2,1)}, bf16[2,192,384]{2,1,0:T(8,128)(2,1)S(1)}, u32[]{:S(2)}, u32[]{:S(2)}) collective-permute-start(bf16[2,192,384]{2,1,0:T(8,128)(2,1)} %add_ring.13.refs_0_), channel_id=1, source_target_pairs={{0,12},{4,0},{8,4},{12,8},{1,13},{5,1},{9,5},{13,9},{2,14},{6,2},{... | collective-permute-start | bytes 884744 | tf_op jit(solution)/shard_map/ppermute | solution.py:363
  222.6 12.6 %collective-permute-start.35 = (bf16[2,192,384]{2,1,0:T(8,128)(2,1)}, bf16[2,192,384]{2,1,0:T(8,128)(2,1)S(1)}, u32[]{:S(2)}, u32[]{:S(2)}) collective-permute-start(bf16[2,192,384]{2,1,0:T(8,128)(2,1)} %add_ring.13.refs_0_), channel_id=1, source_target_pairs={{0,4},{4,8},{8,12},{12,0},{1,5},{5,9},{9,13},{13,1},{2,6},{6,10},{... | collective-permute-start | bytes 884744 | tf_op jit(solution)/shard_map/ppermute | solution.py:363
  222.6 15.5 %collective-permute-start.49 = (bf16[2,192,384]{2,1,0:T(8,128)(2,1)}, bf16[2,192,384]{2,1,0:T(8,128)(2,1)S(1)}, u32[]{:S(2)}, u32[]{:S(2)}) collective-permute-start(bf16[2,192,384]{2,1,0:T(8,128)(2,1)} %add_ring.16.refs_0_), channel_id=1, source_target_pairs={{0,18},{16,0},{2,16},{18,2},{1,19},{17,1},{3,17},{19,3},{4,22},{20... | collective-permute-start | bytes 884744 | tf_op jit(solution)/shard_map/ppermute | solution.py:363
  226.5 11.6 %collective-permute-start.48 = (bf16[2,192,384]{2,1,0:T(8,128)(2,1)}, bf16[2,192,384]{2,1,0:T(8,128)(2,1)S(1)}, u32[]{:S(2)}, u32[]{:S(2)}) collective-permute-start(bf16[2,192,384]{2,1,0:T(8,128)(2,1)} %add_ring.16.refs_0_), channel_id=1, source_target_pairs={{0,2},{16,18},{2,0},{18,16},{1,3},{17,19},{3,1},{19,17},{4,6},{20,... | collective-permute-start | bytes 884744 | tf_op jit(solution)/shard_map/ppermute | solution.py:363
  231.1 11.8 %collective-permute-start.47 = (bf16[2,192,384]{2,1,0:T(8,128)(2,1)}, bf16[2,192,384]{2,1,0:T(8,128)(2,1)S(1)}, u32[]{:S(2)}, u32[]{:S(2)}) collective-permute-start(bf16[2,192,384]{2,1,0:T(8,128)(2,1)} %add_ring.16.refs_0_), channel_id=1, source_target_pairs={{0,16},{16,2},{2,18},{18,0},{1,17},{17,3},{3,19},{19,1},{4,20},{20... | collective-permute-start | bytes 884744 | tf_op jit(solution)/shard_map/ppermute | solution.py:363
  231.1 12.9 %collective-permute-start.53 = (bf16[2,192,384]{2,1,0:T(8,128)(2,1)}, bf16[2,192,384]{2,1,0:T(8,128)(2,1)S(1)}, u32[]{:S(2)}, u32[]{:S(2)}) collective-permute-start(bf16[2,192,384]{2,1,0:T(8,128)(2,1)} %add_ring.11.refs_0_), channel_id=1, source_target_pairs={{0,1},{1,0},{2,3},{3,2},{4,5},{5,4},{6,7},{7,6},{8,9},{9,8},{10,11... | collective-permute-start | bytes 884744 | tf_op jit(solution)/shard_map/ppermute | solution.py:379
  238.1 16.9 %collective-permute-start.26 = (bf16[2,192,384]{2,1,0:T(8,128)(2,1)}, bf16[2,192,384]{2,1,0:T(8,128)(2,1)S(1)}, u32[]{:S(2)}, u32[]{:S(2)}) collective-permute-start(bf16[2,192,384]{2,1,0:T(8,128)(2,1)} %add_ring.11.refs_0_), channel_id=1, source_target_pairs={{0,4},{4,8},{8,12},{12,0},{1,5},{5,9},{9,13},{13,1},{2,6},{6,10},{... | collective-permute-start | bytes 884744 | tf_op jit(solution)/shard_map/ppermute | solution.py:363
  242.9 12.6 %collective-permute-start.57 = (bf16[2,192,384]{2,1,0:T(8,128)(2,1)}, bf16[2,192,384]{2,1,0:T(8,128)(2,1)S(1)}, u32[]{:S(2)}, u32[]{:S(2)}) collective-permute-start(bf16[2,192,384]{2,1,0:T(8,128)(2,1)} %add_ring.14.refs_4_), channel_id=1, source_target_pairs={{0,1},{1,0},{2,3},{3,2},{4,5},{5,4},{6,7},{7,6},{8,9},{9,8},{10,11... | collective-permute-start | bytes 884744 | tf_op jit(solution)/shard_map/ppermute | solution.py:379
  244.1 13.8 %collective-permute-start.40 = (bf16[2,192,384]{2,1,0:T(8,128)(2,1)}, bf16[2,192,384]{2,1,0:T(8,128)(2,1)S(1)}, u32[]{:S(2)}, u32[]{:S(2)}) collective-permute-start(bf16[2,192,384]{2,1,0:T(8,128)(2,1)} %add_ring.14.refs_4_), channel_id=1, source_target_pairs={{0,18},{16,0},{2,16},{18,2},{1,19},{17,1},{3,17},{19,3},{4,22},{20... | collective-permute-start | bytes 884744 | tf_op jit(solution)/shard_map/ppermute | solution.py:363
  248.9 14.3 %collective-permute-start.38 = (bf16[2,192,384]{2,1,0:T(8,128)(2,1)}, bf16[2,192,384]{2,1,0:T(8,128)(2,1)S(1)}, u32[]{:S(2)}, u32[]{:S(2)}) collective-permute-start(bf16[2,192,384]{2,1,0:T(8,128)(2,1)} %add_ring.14.refs_4_), channel_id=1, source_target_pairs={{0,16},{16,2},{2,18},{18,0},{1,17},{17,3},{3,19},{19,1},{4,20},{20... | collective-permute-start | bytes 884744 | tf_op jit(solution)/shard_map/ppermute | solution.py:363
  255.6 15.1 %collective-permute-start.52 = (bf16[2,192,384]{2,1,0:T(8,128)(2,1)}, bf16[2,192,384]{2,1,0:T(8,128)(2,1)S(1)}, u32[]{:S(2)}, u32[]{:S(2)}) collective-permute-start(bf16[2,192,384]{2,1,0:T(8,128)(2,1)} %add_ring.17.refs_8_), channel_id=1, source_target_pairs={{0,96},{32,0},{64,32},{96,64},{1,97},{33,1},{65,33},{97,65},{2,98}... | collective-permute-start | bytes 884744 | tf_op jit(solution)/shard_map/ppermute | solution.py:363
  257.8 13.9 %collective-permute-start.51 = (bf16[2,192,384]{2,1,0:T(8,128)(2,1)}, bf16[2,192,384]{2,1,0:T(8,128)(2,1)S(1)}, u32[]{:S(2)}, u32[]{:S(2)}) collective-permute-start(bf16[2,192,384]{2,1,0:T(8,128)(2,1)} %add_ring.17.refs_8_), channel_id=1, source_target_pairs={{0,64},{32,96},{64,0},{96,32},{1,65},{33,97},{65,1},{97,33},{2,66}... | collective-permute-start | bytes 884744 | tf_op jit(solution)/shard_map/ppermute | solution.py:363
  257.9 16.5 %collective-permute-start.50 = (bf16[2,192,384]{2,1,0:T(8,128)(2,1)}, bf16[2,192,384]{2,1,0:T(8,128)(2,1)S(1)}, u32[]{:S(2)}, u32[]{:S(2)}) collective-permute-start(bf16[2,192,384]{2,1,0:T(8,128)(2,1)} %add_ring.17.refs_8_), channel_id=1, source_target_pairs={{0,32},{32,64},{64,96},{96,0},{1,33},{33,65},{65,97},{97,1},{2,34}... | collective-permute-start | bytes 884744 | tf_op jit(solution)/shard_map/ppermute | solution.py:363
  263.3 11.8 %collective-permute-start.56 = (bf16[2,192,384]{2,1,0:T(8,128)(2,1)S(1)}, bf16[2,192,384]{2,1,0:T(8,128)(2,1)S(1)}, u32[]{:S(2)}, u32[]{:S(2)}) collective-permute-start(bf16[2,192,384]{2,1,0:T(8,128)(2,1)S(1)} %collective-permute-done.28.refs_3_), channel_id=1, source_target_pairs={{0,1},{1,0},{2,3},{3,2},{4,5},{5,4},{6,7},{7,6},{8,9},{9,8},{10,11... | collective-permute-start | bytes 884744 | tf_op jit(solution)/shard_map/ppermute | solution.py:379
  (79 other events, 755.0 us)
